TPU v7x, 32 devices: a whole 2x2x4 slice. The times are simulated.
32 devices in a mesh: dp: 16 (over z, x, core), seq: 2 (over y).
Axes of the slice: x: 2, y: 2, z: 4, core: 2. Of those that a mesh axis runs over, the one named last changes fastest.
Arguments:
- tokens: bfloat16 [16, 256, 1024], P('dp', 'seq'), may hold values from -6 to 6
- segments: int32 [16, 256], P('dp', 'seq'), may hold values from 0 to 5, never falling along the last dimension, each value on 1 to 85 neighbouring positions
- cotangent: bfloat16 [16, 256, 1024], P('dp', 'seq'), may hold values from -6 to 6
- qkv_weight: bfloat16 [1024, 3, 1024], P('dp', None, 'seq')
- out_weight: bfloat16 [1024, 1024], P('seq', 'dp'), may hold values from -1.5 to 1.5
- in_weight: bfloat16 [1024, 2, 2624], P('dp', None, 'seq'), may hold values from -0.1875 to 0.1875
- down_weight: bfloat16 [2624, 1024], P('seq', 'dp'), may hold values from -0.125 to 0.125
- attn_gain: float32 [1024], P('dp'), may hold values from 0.25 to 1.75
- mlp_gain: float32 [1024], P('dp'), may hold values from 0.25 to 1.75
Outputs:
- layer_out: bfloat16 [16, 256, 1024], P('dp', 'seq')
- tokens_grad: bfloat16 [16, 256, 1024], P('dp', 'seq')
- qkv_grad: float32 [1024, 3, 1024], P('dp', None, 'seq')
- out_grad: float32 [1024, 1024], P('seq', 'dp')
- in_grad: float32 [1024, 2, 2624], P('dp', None, 'seq')
- down_grad: float32 [2624, 1024], P('seq', 'dp')
- attn_gain_grad: float32 [1024], P('dp')
- mlp_gain_grad: float32 [1024], P('dp')
Inputs may be any that keep to these rules, and one draw needn't show every extreme that they name: `segments`: along each sequence the numbers never fall; each of the 6 documents has 1 to 85 tokens, and one has exactly 85.
All inputs are finite; a program needn't handle non-finite values.
Results may differ from a plain program's by a relative error of at most 0.034.
Values may be sent and summed in bfloat16 or wider, within the bound.
A program may use at most 128 MiB of HBM per device.

v0:
```python
import math

import jax
import jax.numpy as jnp
from jax import lax
from jax.sharding import PartitionSpec as P

HEADS = 16
HALO = 64


EPS = 1e-05
THETA = 10000.0
NEG_FILL = -1e30


def norm_forward(values, gain):
    center = values - jnp.mean(values, axis=-1, keepdims=True)
    inv_std = lax.rsqrt(jnp.mean(center * center, axis=-1, keepdims=True) + EPS)
    unit_rows = center * inv_std
    return (unit_rows * gain, unit_rows, inv_std)


def norm_backward(grad_rows, gain, unit_rows, inv_std):
    scaled = grad_rows * gain
    inner = (
        scaled
        - jnp.mean(scaled, axis=-1, keepdims=True)
        - unit_rows * jnp.mean(scaled * unit_rows, axis=-1, keepdims=True)
    )
    return (inner * inv_std, jnp.sum(grad_rows * unit_rows, axis=0))


def gelu_value(inputs):
    return 0.5 * inputs * (1.0 + lax.erf(inputs * 0.7071067811865476))


def gelu_slope(inputs):
    return (
        0.5 * (1.0 + lax.erf(inputs * 0.7071067811865476))
        + inputs * jnp.exp(-0.5 * inputs * inputs) * 0.3989422804014327
    )


def rotary_tables(positions, head_size):
    half_size = head_size // 2
    freqs = jnp.power(THETA, -(2.0 / head_size) * jnp.arange(half_size, dtype=jnp.float32))
    angles = positions.astype(jnp.float32)[:, None] * freqs[None, :]
    return (jnp.cos(angles)[:, None, :], jnp.sin(angles)[:, None, :])


def rotate(values, cos_table, sin_table):
    half_size = values.shape[-1] // 2
    lower_half = values[..., :half_size]
    upper_half = values[..., half_size:]
    return jnp.concatenate(
        [
            lower_half * cos_table - upper_half * sin_table,
            upper_half * cos_table + lower_half * sin_table,
        ],
        axis=-1,
    )


def unrotate(grads, cos_table, sin_table):
    half_size = grads.shape[-1] // 2
    lower_half = grads[..., :half_size]
    upper_half = grads[..., half_size:]
    return jnp.concatenate(
        [
            lower_half * cos_table + upper_half * sin_table,
            upper_half * cos_table - lower_half * sin_table,
        ],
        axis=-1,
    )


def window_mask(query_pos, key_pos, query_seg, key_seg, halo_width, total_len):
    near = jnp.abs(query_pos[:, None] - key_pos[None, :]) <= halo_width
    inside = (key_pos >= 0) & (key_pos < total_len)
    return near & inside[None, :] & (query_seg[:, None] == key_seg[None, :])


def block_scores(queries, key_slab, allowed, scale):
    scores = (
        jnp.einsum("qhd,khd->hqk", queries, key_slab, preferred_element_type=jnp.float32) * scale
    )
    return jnp.where(allowed[None], scores, NEG_FILL)


def attend_block(queries, key_slab, value_slab, allowed, scale):
    scores = block_scores(queries, key_slab, allowed, scale)
    top_score = jnp.max(scores, axis=-1, keepdims=True)
    total = jnp.sum(jnp.exp(scores - top_score), axis=-1, keepdims=True)
    logsum = top_score + jnp.log(total)
    probs = jnp.exp(scores - logsum).astype(jnp.bfloat16)
    mixed = jnp.einsum("hqk,khd->qhd", probs, value_slab, preferred_element_type=jnp.float32)
    return (mixed, logsum[..., 0])


def attend_back(queries, key_slab, value_slab, allowed, scale, logsum, mixed_b, dmixed_b):
    scores = block_scores(queries, key_slab, allowed, scale)
    probs = jnp.exp(scores - logsum[..., None])
    probs_b = probs.astype(jnp.bfloat16)
    dvalues = jnp.einsum("hqk,qhd->khd", probs_b, dmixed_b, preferred_element_type=jnp.float32)
    dprobs = jnp.einsum("qhd,khd->hqk", dmixed_b, value_slab, preferred_element_type=jnp.float32)
    delta = jnp.transpose(
        jnp.sum(dmixed_b.astype(jnp.float32) * mixed_b.astype(jnp.float32), axis=-1)
    )
    dscores = (probs * (dprobs - delta[..., None]) * scale).astype(jnp.bfloat16)
    dqueries = jnp.einsum("hqk,khd->qhd", dscores, key_slab, preferred_element_type=jnp.float32)
    dkeys = jnp.einsum("hqk,qhd->khd", dscores, queries, preferred_element_type=jnp.float32)
    return (dqueries, dkeys, dvalues)


def per_device(
    tokens, segments, cotangent, qkv_weight, out_weight, in_weight, down_weight, attn_gain, mlp_gain
):
    full_qkv, full_out, full_in, full_down, gain_attn, gain_mlp = (
        lax.all_gather(qkv_weight, "dp", axis=0, tiled=True),
        lax.all_gather(out_weight, "dp", axis=1, tiled=True),
        lax.all_gather(in_weight, "dp", axis=0, tiled=True),
        lax.all_gather(down_weight, "dp", axis=1, tiled=True),
        lax.all_gather(attn_gain.astype(jnp.bfloat16), "dp", axis=0, tiled=True).astype(
            attn_gain.dtype
        ),
        lax.all_gather(mlp_gain.astype(jnp.bfloat16), "dp", axis=0, tiled=True).astype(
            mlp_gain.dtype
        ),
    )
    layer_in = tokens[0]
    seg_local = segments[0]
    cot_local = cotangent[0]
    model_width = layer_in.shape[1]
    head_size = model_width // HEADS
    local_width = full_qkv.shape[2]
    local_heads = local_width // head_size
    local_hidden = full_in.shape[2]
    halo_width = HALO
    scale = 1.0 / math.sqrt(head_size)
    inputs32 = layer_in.astype(jnp.float32)
    normed_one, unit_one, inv_one = norm_forward(inputs32, gain_attn)
    normed_one_b = normed_one.astype(jnp.bfloat16)
    normed_full, cot_full, seg_gathered = (
        lax.all_gather(normed_one_b, "seq", axis=0, tiled=True),
        lax.all_gather(cot_local, "seq", axis=0, tiled=True),
        lax.all_gather(seg_local.astype(jnp.bfloat16), "seq", axis=0, tiled=True),
    )
    seg_full = seg_gathered.astype(jnp.int32)
    total_len = normed_full.shape[0]
    block_rows = min(total_len, 512)
    slab_rows = block_rows + 2 * halo_width
    projected = jnp.dot(
        normed_full,
        full_qkv.reshape(model_width, 3 * local_width),
        preferred_element_type=jnp.float32,
    )
    positions = jnp.arange(total_len, dtype=jnp.int32)
    cos_table, sin_table = rotary_tables(positions, head_size)
    queries = rotate(
        projected[:, :local_width].reshape(total_len, local_heads, head_size), cos_table, sin_table
    ).astype(jnp.bfloat16)
    keys_rot = rotate(
        projected[:, local_width : 2 * local_width].reshape(total_len, local_heads, head_size),
        cos_table,
        sin_table,
    ).astype(jnp.bfloat16)
    values_b = (
        projected[:, 2 * local_width :]
        .reshape(total_len, local_heads, head_size)
        .astype(jnp.bfloat16)
    )
    pad_spec = ((halo_width, halo_width), (0, 0), (0, 0))
    key_pad = jnp.pad(keys_rot, pad_spec)
    value_pad = jnp.pad(values_b, pad_spec)
    seg_pad = jnp.pad(seg_full, (halo_width, halo_width), constant_values=-1)
    mixed_parts = []
    logsum_parts = []
    masks = []
    for start in range(0, total_len, block_rows):
        query_pos = start + jnp.arange(block_rows, dtype=jnp.int32)
        key_pos = start - halo_width + jnp.arange(slab_rows, dtype=jnp.int32)
        allowed = window_mask(
            query_pos,
            key_pos,
            seg_full[start : start + block_rows],
            seg_pad[start : start + slab_rows],
            halo_width,
            total_len,
        )
        masks.append(allowed)
        mixed_part, logsum_part = attend_block(
            queries[start : start + block_rows],
            key_pad[start : start + slab_rows],
            value_pad[start : start + slab_rows],
            allowed,
            scale,
        )
        mixed_parts.append(mixed_part)
        logsum_parts.append(logsum_part)
    mixed_b = jnp.concatenate(mixed_parts, axis=0).astype(jnp.bfloat16)
    mixed_flat = mixed_b.reshape(total_len, local_width)
    rows = mixed_flat
    residual = inputs32 + lax.psum_scatter(
        jnp.dot(rows, full_out, preferred_element_type=jnp.float32).astype(jnp.bfloat16),
        "seq",
        scatter_dimension=0,
        tiled=True,
    ).astype(jnp.float32)
    normed_two, unit_two, inv_two = norm_forward(residual, gain_mlp)
    normed_two_b = normed_two.astype(jnp.bfloat16)
    normed_two_full = lax.all_gather(normed_two_b, "seq", axis=0, tiled=True)
    in_flat = full_in.reshape(model_width, 2 * local_hidden)
    gate_parts = []
    linear_parts = []
    for start in range(0, total_len, block_rows):
        expanded = jnp.dot(
            normed_two_full[start : start + block_rows], in_flat, preferred_element_type=jnp.float32
        )
        gate_parts.append(expanded[:, :local_hidden])
        linear_parts.append(expanded[:, local_hidden:])
    gate_in = jnp.concatenate(gate_parts, axis=0)
    linear_in = jnp.concatenate(linear_parts, axis=0)
    activated = gelu_value(gate_in)
    middle_b = (activated * linear_in).astype(jnp.bfloat16)
    rows = middle_b
    layer_out = (
        residual
        + lax.psum_scatter(
            jnp.dot(rows, full_down, preferred_element_type=jnp.float32).astype(jnp.bfloat16),
            "seq",
            scatter_dimension=0,
            tiled=True,
        ).astype(jnp.float32)
    ).astype(jnp.bfloat16)
    back_qkv, back_out, back_in, back_down, back_gain_attn, back_gain_mlp = (
        lax.all_gather(qkv_weight, "dp", axis=0, tiled=True),
        lax.all_gather(out_weight, "dp", axis=1, tiled=True),
        lax.all_gather(in_weight, "dp", axis=0, tiled=True),
        lax.all_gather(down_weight, "dp", axis=1, tiled=True),
        lax.all_gather(attn_gain.astype(jnp.bfloat16), "dp", axis=0, tiled=True).astype(
            attn_gain.dtype
        ),
        lax.all_gather(mlp_gain.astype(jnp.bfloat16), "dp", axis=0, tiled=True).astype(
            mlp_gain.dtype
        ),
    )
    back_in_flat = back_in.reshape(model_width, 2 * local_hidden)
    back_qkv_flat = back_qkv.reshape(model_width, 3 * local_width)
    down_grad = jnp.dot(middle_b.T, cot_full, preferred_element_type=jnp.float32)
    dmiddle = jnp.dot(cot_full, back_down.T, preferred_element_type=jnp.float32)
    dexpanded_b = jnp.concatenate(
        [dmiddle * linear_in * gelu_slope(gate_in), dmiddle * activated], axis=1
    ).astype(jnp.bfloat16)
    in_grad = jnp.dot(normed_two_full.T, dexpanded_b, preferred_element_type=jnp.float32).reshape(
        model_width, 2, local_hidden
    )
    rows = dexpanded_b
    dnormed_two = lax.psum_scatter(
        jnp.dot(rows, back_in_flat.T, preferred_element_type=jnp.float32).astype(jnp.bfloat16),
        "seq",
        scatter_dimension=0,
        tiled=True,
    ).astype(jnp.float32)
    dres_norm, mlp_gain_part = norm_backward(dnormed_two, back_gain_mlp, unit_two, inv_two)
    dresidual = cot_local.astype(jnp.float32) + dres_norm
    dresidual_b = dresidual.astype(jnp.bfloat16)
    dres_full = lax.all_gather(dresidual_b, "seq", axis=0, tiled=True)
    out_grad = jnp.dot(mixed_flat.T, dres_full, preferred_element_type=jnp.float32)
    dmixed_b = (
        jnp.dot(dres_full, back_out.T, preferred_element_type=jnp.float32)
        .astype(jnp.bfloat16)
        .reshape(total_len, local_heads, head_size)
    )
    dkey_pad = jnp.zeros((total_len + 2 * halo_width, local_heads, head_size), jnp.float32)
    dvalue_pad = jnp.zeros((total_len + 2 * halo_width, local_heads, head_size), jnp.float32)
    dquery_parts = []
    for index, start in enumerate(range(0, total_len, block_rows)):
        dqueries, dkeys, dvalues = attend_back(
            queries[start : start + block_rows],
            key_pad[start : start + slab_rows],
            value_pad[start : start + slab_rows],
            masks[index],
            scale,
            logsum_parts[index],
            mixed_b[start : start + block_rows],
            dmixed_b[start : start + block_rows],
        )
        dquery_parts.append(dqueries)
        dkey_pad = dkey_pad.at[start : start + slab_rows].add(dkeys)
        dvalue_pad = dvalue_pad.at[start : start + slab_rows].add(dvalues)
    dquery_all = unrotate(jnp.concatenate(dquery_parts, axis=0), cos_table, sin_table).reshape(
        total_len, local_width
    )
    dkey_all = unrotate(
        dkey_pad[halo_width : halo_width + total_len], cos_table, sin_table
    ).reshape(total_len, local_width)
    dvalue_all = dvalue_pad[halo_width : halo_width + total_len].reshape(total_len, local_width)
    dqkv_b = jnp.concatenate([dquery_all, dkey_all, dvalue_all], axis=1).astype(jnp.bfloat16)
    qkv_grad = jnp.dot(normed_full.T, dqkv_b, preferred_element_type=jnp.float32).reshape(
        model_width, 3, local_width
    )
    rows = dqkv_b
    dnormed_one = lax.psum_scatter(
        jnp.dot(rows, back_qkv_flat.T, preferred_element_type=jnp.float32).astype(jnp.bfloat16),
        "seq",
        scatter_dimension=0,
        tiled=True,
    ).astype(jnp.float32)
    dinput_norm, attn_gain_part = norm_backward(dnormed_one, back_gain_attn, unit_one, inv_one)
    tokens_grad = (dresidual + dinput_norm).astype(jnp.bfloat16)
    attn_gain_sum, mlp_gain_sum = lax.psum((attn_gain_part, mlp_gain_part), "seq")
    qkv_share, out_share, in_share, down_share, attn_gain_share, mlp_gain_share = (
        lax.psum_scatter(
            qkv_grad.astype(jnp.bfloat16), "dp", scatter_dimension=0, tiled=True
        ).astype(jnp.float32),
        lax.psum_scatter(
            out_grad.astype(jnp.bfloat16), "dp", scatter_dimension=1, tiled=True
        ).astype(jnp.float32),
        lax.psum_scatter(
            in_grad.astype(jnp.bfloat16), "dp", scatter_dimension=0, tiled=True
        ).astype(jnp.float32),
        lax.psum_scatter(
            down_grad.astype(jnp.bfloat16), "dp", scatter_dimension=1, tiled=True
        ).astype(jnp.float32),
        lax.psum_scatter(
            attn_gain_sum.astype(jnp.bfloat16), "dp", scatter_dimension=0, tiled=True
        ).astype(jnp.float32),
        lax.psum_scatter(
            mlp_gain_sum.astype(jnp.bfloat16), "dp", scatter_dimension=0, tiled=True
        ).astype(jnp.float32),
    )
    return (
        layer_out[None],
        tokens_grad[None],
        qkv_share,
        out_share,
        in_share,
        down_share,
        attn_gain_share,
        mlp_gain_share,
    )


def solution(mesh):
    return jax.shard_map(
        per_device,
        mesh=mesh,
        in_specs=(
            P("dp", "seq", None),
            P("dp", "seq"),
            P("dp", "seq", None),
            P("dp", None, "seq"),
            P("seq", "dp"),
            P("dp", None, "seq"),
            P("seq", "dp"),
            P("dp"),
            P("dp"),
        ),
        out_specs=(
            P("dp", "seq", None),
            P("dp", "seq", None),
            P("dp", None, "seq"),
            P("seq", "dp"),
            P("dp", None, "seq"),
            P("seq", "dp"),
            P("dp"),
            P("dp"),
        ),
        check_vma=False,
    )
```

profile of v0, /device:TPU:0, one launch (start us, length us, event | category | flops | bytes accessed | tf_op | source)
XLA Modules:
  0.0 637.5 jit_solution(9426439506125816171)
XLA Ops:
  9.4 5.2 all-gather
  20.6 33.5 %all-reduce.11 = (bf16[1024]{0:T(1024)(128)(2,1)S(1)}, bf16[1024]{0:T(1024)(128)(2,1)S(1)}) all-reduce(bf16[1024]{0:T(1024)(128)(2,1)S(1)} %dynamic-update-slice.5, bf16[1024]{0:T(1024)(128)(2,1)S(1)} %dynamic-update-slice.4), channel_id=1, replica_groups=mesh['dp'=16,'seq'=2] {'dp'}, use_global_device_ids=true, to_apply=%add.4 | all-reduce | flops 2048 | bytes 8192
  55.3 7.1 %all_gather.40 = bf16[256,1024]{1,0:T(8,128)(2,1)} all-gather(bf16[128,1024]{1,0:T(8,128)(2,1)S(1)} %fusion.24), channel_id=1, replica_groups=mesh['dp'=16,'seq'=2] {'seq'}, dimensions={0}, use_global_device_ids=true | all-gather | bytes 786432 | tf_op jit(solution)/shard_map/all_gather | solution.py:145
  64.2 3.2 copy.34
  67.4 2.1 fusion.64
  82.8 14.1 %all-gather.9.cloned.1.call-done = bf16[512,1024]{0,1:T(8,128)(2,1)} async-done(((bf16[512,64]{0,1:T(8,128)(2,1)}), bf16[512,1024]{0,1:T(8,128)(2,1)}) %all-gather.9.cloned.1.call-update) | async-done | bytes 1048592 | tf_op jit(solution)/shard_map/all_gather | solution.py:121
  96.8 2.6 convolution_convert_fusion.4
  100.7 16.0 %all-gather.1 = bf16[1,256,1024]{2,1,0:T(8,128)(2,1)} all-gather(bf16[1,128,1024]{2,1,0:T(8,128)(2,1)} %param.19), channel_id=3, replica_groups=mesh['dp'=16,'seq'=2] {'seq'}, dimensions={1}, use_global_device_ids=true | all-gather | bytes 786432 | tf_op jit(solution)/shard_map/all_gather | solution.py:146
  121.5 9.1 %all_gather.45 = bf16[256,1024]{1,0:T(8,128)(2,1)} all-gather(bf16[128,1024]{1,0:T(8,128)(2,1)S(1)} %multiply_convert_fusion.3), channel_id=1, replica_groups=mesh['dp'=16,'seq'=2] {'seq'}, dimensions={0}, use_global_device_ids=true | all-gather | bytes 786432 | tf_op jit(solution)/shard_map/all_gather | solution.py:212
  130.6 46.4 %all-gather.11.cloned.1.call-done = bf16[1024,2,1312]{2,1,0:T(2,128)(2,1)} async-done(((bf16[64,2,1312]{2,1,0:T(2,128)(2,1)}), bf16[1024,2,1312]{2,1,0:T(2,128)(2,1)}) %all-gather.11.cloned.1.call-update) | async-done | bytes 5373968 | tf_op jit(solution)/shard_map/all_gather | solution.py:122
  177.0 14.9 %copy.38 = bf16[1024,2,1312]{0,2,1:T(8,128)(2,1)} copy(bf16[1024,2,1312]{2,1,0:T(2,128)(2,1)} %all-gather.11.cloned.1.call-done) | data formatting | bytes 10747904 | tf_op jit(solution)/shard_map/all_gather | solution.py:122
  191.9 5.8 fusion.65
  197.7 24.1 %all-gather.13.cloned.1.call-done = bf16[1312,1024]{0,1:T(8,128)(2,1)} async-done(((bf16[1312,64]{0,1:T(8,128)(2,1)}), bf16[1312,1024]{0,1:T(8,128)(2,1)}) %all-gather.13.cloned.1.call-update) | async-done | bytes 2686992 | tf_op jit(solution)/shard_map/all_gather | solution.py:123
  221.8 5.5 fusion.7
  228.3 2.5 convolution_convert_fusion.7
  230.9 13.4 %reduce-scatter.11.cloned.1.call-done = bf16[128,1024]{1,0:T(8,128)(2,1)} async-done(((bf16[256,1024]{1,0:T(8,128)(2,1)}), bf16[128,1024]{1,0:T(8,128)(2,1)}) %reduce-scatter.11.cloned.1.call-update) | async-done | bytes 262160 | tf_op jit(solution)/shard_map/reduce_scatter | solution.py:259
  247.1 8.6 %all_gather.49 = bf16[256,1024]{1,0:T(8,128)(2,1)S(1)} all-gather(bf16[128,1024]{1,0:T(8,128)(2,1)S(1)} %fusion.61), channel_id=1, replica_groups=mesh['dp'=16,'seq'=2] {'seq'}, dimensions={0}, use_global_device_ids=true | all-gather | bytes 786432 | tf_op jit(solution)/shard_map/all_gather | solution.py:268
  260.7 2.8 fusion.8
  269.6 3.9 convolution_convert_fusion.5
  275.3 2.6 convolution_convert_fusion.1
  279.3 4.0 convolution_convert_fusion
  283.3 15.0 %copy.42 = bf16[1024,2,1312]{2,1,0:T(2,128)(2,1)} copy(bf16[1024,2,1312]{0,2,1:T(8,128)(2,1)} %bitcast.122) | data formatting | bytes 10747904 | tf_op jit(solution)/shard_map/convert_element_type | solution.py:321
  298.3 2.3 convolution_convert_fusion.2
  300.6 2.9 copy.40
  303.6 7.6 %copy.41 = bf16[1024,3,512]{2,1,0:T(4,128)(2,1)} copy(bf16[1024,3,512]{0,2,1:T(8,128)(2,1)} %bitcast.123) | data formatting | bytes 6291456 | tf_op jit(solution)/shard_map/convert_element_type | solution.py:315
  313.3 5.0 all-reduce.9
  318.3 31.1 %all-reduce.10 = (bf16[1024]{0:T(1024)(128)(2,1)S(1)}, bf16[1024]{0:T(1024)(128)(2,1)S(1)}) all-reduce(bf16[1024]{0:T(1024)(128)(2,1)S(1)} %get-tuple-element.70, bf16[1024]{0:T(1024)(128)(2,1)S(1)} %get-tuple-element.71), channel_id=12, replica_groups=mesh['dp'=16,'seq'=2] {'dp'}, use_global_device_ids=true, to_apply=%region_21.22.clone | all-reduce | flops 2048 | bytes 8192
  350.6 2.3 fusion.47
  352.9 9.8 %reduce-scatter.15.cloned.1.call-done = bf16[512,64]{0,1:T(8,128)(2,1)} async-done(((bf16[512,1024]{0,1:T(8,128)(2,1)}), bf16[512,64]{0,1:T(8,128)(2,1)}) %reduce-scatter.15.cloned.1.call-update) | async-done | bytes 65552 | tf_op jit(solution)/shard_map/reduce_scatter | solution.py:317
  364.2 66.3 %reduce-scatter.17.cloned.1.call-done = bf16[1312,64]{0,1:T(8,128)(2,1)} async-done(((bf16[1312,1024]{0,1:T(8,128)(2,1)}), bf16[1312,64]{0,1:T(8,128)(2,1)}) %reduce-scatter.17.cloned.1.call-update) | async-done | bytes 167952 | tf_op jit(solution)/shard_map/reduce_scatter | solution.py:323
  432.2 194.8 %all-reduce.15.cloned.1.call-done = (bf16[1024,3,512]{2,1,0:T(4,128)(2,1)}, bf16[1024,2,1312]{2,1,0:T(2,128)(2,1)}) async-done(((bf16[1024,3,512]{2,1,0:T(4,128)(2,1)}, bf16[1024,2,1312]{2,1,0:T(2,128)(2,1)}), (bf16[1024,3,512]{2,1,0:T(4,128)(2,1)}, bf16[1024,2,1312]{2,1,0:T(2,128)(2,1)})) %all-reduce.15.cloned.1.call-update) | async-done | bytes 8519696
  628.0 2.1 dynamic-slice_convert_fusion
  (180 shorter events, 55.1 us)
Async XLA Ops:
  7.2 57.0 %all-gather.7.cloned.1.call-start = ((), (), s32[]{:S(2)}) async-start(), calls=%async_computation.6 | async-start | bytes 3342336 | tf_op jit(solution)/shard_map/all_gather | solution.py:120
  7.9 88.9 %all-gather.9.cloned.1.call-start = ((), (), s32[]{:S(2)}) async-start(), calls=%async_computation.7 | async-start | bytes 1114112 | tf_op jit(solution)/shard_map/all_gather | solution.py:121
  8.6 109.4 %reduce-scatter.7.cloned.1.call-start = ((), (), s32[]{:S(2)}) async-start(), calls=%async_computation.8 | async-start | bytes 786432 | tf_op jit(solution)/shard_map/reduce_scatter | solution.py:204
  17.0 47.2 %copy-start.38 = (f32[128]{0:T(128)}, f32[128]{0:T(128)S(1)}, u32[]{:S(2)}) copy-start(f32[128]{0:T(128)S(1)} %broadcast_multiply_fusion.5) | copy-start | bytes 1540
  18.2 46.0 %copy-start.44 = (f32[128]{0:T(128)}, f32[128]{0:T(128)S(1)}, u32[]{:S(2)}) copy-start(f32[128]{0:T(128)S(1)} %add_rsqrt_fusion.1) | copy-start | bytes 1540
  82.8 35.3 %copy-start = (bf16[1,128,1024]{2,1,0:T(8,128)(2,1)S(1)}, bf16[1,128,1024]{2,1,0:T(8,128)(2,1)}, u32[]{:S(2)}) copy-start(bf16[1,128,1024]{2,1,0:T(8,128)(2,1)} %param.17) | copy-start | bytes 786436
  99.5 77.5 %all-gather.11.cloned.1.call-start = ((), (), s32[]{:S(2)}) async-start(), calls=%async_computation.9 | async-start | bytes 6127616 | tf_op jit(solution)/shard_map/all_gather | solution.py:122
  100.0 121.7 %all-gather.13.cloned.1.call-start = ((), (), s32[]{:S(2)}) async-start(), calls=%async_computation.10 | async-start | bytes 3063808 | tf_op jit(solution)/shard_map/all_gather | solution.py:123
  100.6 143.6 %reduce-scatter.11.cloned.1.call-start = ((), (), s32[]{:S(2)}) async-start(), calls=%async_computation.12 | async-start | bytes 786432 | tf_op jit(solution)/shard_map/reduce_scatter | solution.py:259
  120.4 71.5 %copy-start.36 = (f32[128]{0:T(128)}, f32[128]{0:T(128)S(1)}, u32[]{:S(2)}) copy-start(f32[128]{0:T(128)S(1)} %add_rsqrt_fusion) | copy-start | bytes 1540
  221.8 6.6 %copy-start.2 = (bf16[1024,2,1312]{0,2,1:T(8,128)(2,1)S(1)}, bf16[1024,2,1312]{0,2,1:T(8,128)(2,1)}, u32[]{:S(2)}) copy-start(bf16[1024,2,1312]{0,2,1:T(8,128)(2,1)} %copy.38) | copy-start | bytes 16121860
  230.8 81.2 %reduce-scatter.13.cloned.1.call-start = ((), (), s32[]{:S(2)}) async-start(), calls=%async_computation.13 | async-start | bytes 786432 | tf_op jit(solution)/shard_map/reduce_scatter | solution.py:304
  244.2 12.2 %copy-start.5 = (bf16[512,1024]{0,1:T(8,128)(2,1)S(1)}, bf16[512,1024]{0,1:T(8,128)(2,1)}, u32[]{:S(2)}) copy-start(bf16[512,1024]{0,1:T(8,128)(2,1)} %all-gather.9.cloned.1.call-done) | copy-start | bytes 3145732
  245.7 10.0 %copy-start.40 = (f32[128]{0:T(128)}, f32[128]{0:T(128)S(1)}, u32[]{:S(2)}) copy-start(f32[128]{0:T(128)S(1)} %get-tuple-element.103) | copy-start | bytes 1540
  245.7 10.0 %copy-start.42 = (f32[128]{0:T(128)}, f32[128]{0:T(128)S(1)}, u32[]{:S(2)}) copy-start(f32[128]{0:T(128)S(1)} %get-tuple-element.104) | copy-start | bytes 1540
  259.4 4.1 copy-start.7
  259.4 4.2 copy-start.17
  259.4 4.2 copy-start.25
  259.4 4.2 copy-start.29
  259.4 4.2 copy-start.35
  269.6 4.1 copy-start.4
  269.6 4.1 copy-start.9
  269.6 81.0 %reduce-scatter.9.cloned.1.call-start = ((), (), s32[]{:S(2)}) async-start(), calls=%async_computation.11 | async-start | bytes 786432 | tf_op jit(solution)/shard_map/reduce_scatter | solution.py:229
  273.6 89.1 %reduce-scatter.15.cloned.1.call-start = ((), (), s32[]{:S(2)}) async-start(), calls=%async_computation.14 | async-start | bytes 1114112 | tf_op jit(solution)/shard_map/reduce_scatter | solution.py:317
  275.2 155.4 %reduce-scatter.17.cloned.1.call-start = ((), (), s32[]{:S(2)}) async-start(), calls=%async_computation.15 | async-start | bytes 3063808 | tf_op jit(solution)/shard_map/reduce_scatter | solution.py:323
  277.9 349.1 %all-reduce.15.cloned.1.call-start = ((), (), s32[]{:S(2)}) async-start(), calls=%async_computation.16 | async-start | bytes 19922944
  311.2 39.4 %copy-start.1 = (bf16[128,1024]{1,0:T(8,128)(2,1)S(1)}, bf16[128,1024]{1,0:T(8,128)(2,1)}, u32[]{:S(2)}) copy-start(bf16[128,1024]{1,0:T(8,128)(2,1)} %reduce-scatter.7.cloned.1.call-done) | copy-start | bytes 786436
  311.2 39.4 %copy-start.10 = (bf16[1,128,1024]{2,1,0:T(8,128)(2,1)S(1)}, bf16[1,128,1024]{2,1,0:T(8,128)(2,1)}, u32[]{:S(2)}) copy-start(bf16[1,128,1024]{2,1,0:T(8,128)(2,1)} %param.19) | copy-start | bytes 786436
  311.2 39.4 %copy-start.11 = (bf16[128,1024]{1,0:T(8,128)(2,1)S(1)}, bf16[128,1024]{1,0:T(8,128)(2,1)}, u32[]{:S(2)}) copy-start(bf16[128,1024]{1,0:T(8,128)(2,1)} %reduce-scatter.11.cloned.1.call-done) | copy-start | bytes 786436
  311.2 39.4 %copy-start.37 = (f32[128]{0:T(128)S(1)}, f32[128]{0:T(128)}, u32[]{:S(2)}) copy-start(f32[128]{0:T(128)} %copy-done.36) | copy-start | bytes 1540
  311.2 39.4 %copy-start.41 = (f32[128]{0:T(128)S(1)}, f32[128]{0:T(128)}, u32[]{:S(2)}) copy-start(f32[128]{0:T(128)} %copy-done.40) | copy-start | bytes 1540
  311.3 39.4 %copy-start.43 = (f32[128]{0:T(128)S(1)}, f32[128]{0:T(128)}, u32[]{:S(2)}) copy-start(f32[128]{0:T(128)} %copy-done.42) | copy-start | bytes 1540
  (25 other events, 33.7 us)
Sparse Core Ops, SparseCore 0:
  10.2 48.0 all-gather.6
  60.4 36.4 all-gather.8
  99.7 18.3 reduce-scatter.6
  120.2 56.7 all-gather.10
  179.1 42.6 all-gather.12
  230.9 13.2 reduce-scatter.10
  269.7 14.6 reduce-scatter.12
  286.6 14.6 reduce-scatter.8
  304.9 57.7 reduce-scatter.14
  366.4 64.1 reduce-scatter.16
  434.4 192.6 all-reduce.14
where the time goes:
time: 640 us; the launch traced here: 638 us
  waiting for transfers between devices  373 us (58%)
  blocking collectives  116 us (18%)
  local copies, waits for them, and re-layouts  59.6 us (9%)
  matrix products  44.6 us (7%)
  other arithmetic  28.3 us (4%)
  between operations  15.9 us (2%)
    unnamed x12, waiting for transfers between devices  197 us
    reduce_scatter x1, waiting for transfers between devices, per_device(): lax.psum_scatter(down_grad.astype(jnp.bfloat16), 'dp', scatter_dimension=...  66.3 us
    unnamed x2, blocking collectives  64.6 us
    all_gather x1, waiting for transfers between devices, per_device(): lax.all_gather(in_weight, 'dp', axis=0, tiled=True)  46.4 us
    all_gather x1, waiting for transfers between devices, per_device(): lax.all_gather(down_weight, 'dp', axis=1, tiled=True)  24.1 us
    all_gather x1, blocking collectives, per_device(): lax.all_gather(cot_local, 'seq', axis=0, tiled=True)  16 us
    convert_element_type x1, local copies, waits for them, and re-layouts, per_device(): in_grad.astype(jnp.bfloat16)  15 us
    all_gather x1, local copies, waits for them, and re-layouts, per_device(): lax.all_gather(in_weight, 'dp', axis=0, tiled=True)  14.9 us
  transfers between devices with their start and end apart: 11, of which 8 were waited for; matrix products, arithmetic and copies ran while one was open for 15% of the time, Pallas kernels for 0%

commit v1 on v0

v1 whole, which is shorter than its diff:
```python
import functools
import math

import jax
import jax.numpy as jnp
from jax import lax
from jax.experimental import pallas as pl
from jax.experimental.pallas import tpu as pltpu
from jax.sharding import PartitionSpec as P

HEADS = 16
HALO = 64


EPS = 1e-05
THETA = 10000.0
NEG_FILL = -1e30


def norm_forward(values, gain):
    center = values - jnp.mean(values, axis=-1, keepdims=True)
    inv_std = lax.rsqrt(jnp.mean(center * center, axis=-1, keepdims=True) + EPS)
    unit_rows = center * inv_std
    return (unit_rows * gain, unit_rows, inv_std)


def norm_backward(grad_rows, gain, unit_rows, inv_std):
    scaled = grad_rows * gain
    inner = (
        scaled
        - jnp.mean(scaled, axis=-1, keepdims=True)
        - unit_rows * jnp.mean(scaled * unit_rows, axis=-1, keepdims=True)
    )
    return (inner * inv_std, jnp.sum(grad_rows * unit_rows, axis=0))


def gelu_value(inputs):
    return 0.5 * inputs * (1.0 + lax.erf(inputs * 0.7071067811865476))


def gelu_slope(inputs):
    return (
        0.5 * (1.0 + lax.erf(inputs * 0.7071067811865476))
        + inputs * jnp.exp(-0.5 * inputs * inputs) * 0.3989422804014327
    )


def rotary_tables(positions, head_size):
    half_size = head_size // 2
    freqs = jnp.power(THETA, -(2.0 / head_size) * jnp.arange(half_size, dtype=jnp.float32))
    angles = positions.astype(jnp.float32)[:, None] * freqs[None, :]
    return (jnp.cos(angles)[:, None, :], jnp.sin(angles)[:, None, :])


def rotate(values, cos_table, sin_table):
    half_size = values.shape[-1] // 2
    lower_half = values[..., :half_size]
    upper_half = values[..., half_size:]
    return jnp.concatenate(
        [
            lower_half * cos_table - upper_half * sin_table,
            upper_half * cos_table + lower_half * sin_table,
        ],
        axis=-1,
    )


def unrotate(grads, cos_table, sin_table):
    half_size = grads.shape[-1] // 2
    lower_half = grads[..., :half_size]
    upper_half = grads[..., half_size:]
    return jnp.concatenate(
        [
            lower_half * cos_table + upper_half * sin_table,
            upper_half * cos_table - lower_half * sin_table,
        ],
        axis=-1,
    )


def window_mask(query_pos, key_pos, query_seg, key_seg, halo_width, total_len):
    near = jnp.abs(query_pos[:, None] - key_pos[None, :]) <= halo_width
    inside = (key_pos >= 0) & (key_pos < total_len)
    return near & inside[None, :] & (query_seg[:, None] == key_seg[None, :])


def block_scores(queries, key_slab, allowed, scale):
    scores = (
        jnp.einsum("qhd,khd->hqk", queries, key_slab, preferred_element_type=jnp.float32) * scale
    )
    return jnp.where(allowed[None], scores, NEG_FILL)


def attend_block(queries, key_slab, value_slab, allowed, scale):
    scores = block_scores(queries, key_slab, allowed, scale)
    top_score = jnp.max(scores, axis=-1, keepdims=True)
    total = jnp.sum(jnp.exp(scores - top_score), axis=-1, keepdims=True)
    logsum = top_score + jnp.log(total)
    probs = jnp.exp(scores - logsum).astype(jnp.bfloat16)
    mixed = jnp.einsum("hqk,khd->qhd", probs, value_slab, preferred_element_type=jnp.float32)
    return (mixed, logsum[..., 0])


def attend_back(queries, key_slab, value_slab, allowed, scale, logsum, mixed_b, dmixed_b):
    scores = block_scores(queries, key_slab, allowed, scale)
    probs = jnp.exp(scores - logsum[..., None])
    probs_b = probs.astype(jnp.bfloat16)
    dvalues = jnp.einsum("hqk,qhd->khd", probs_b, dmixed_b, preferred_element_type=jnp.float32)
    dprobs = jnp.einsum("qhd,khd->hqk", dmixed_b, value_slab, preferred_element_type=jnp.float32)
    delta = jnp.transpose(
        jnp.sum(dmixed_b.astype(jnp.float32) * mixed_b.astype(jnp.float32), axis=-1)
    )
    dscores = (probs * (dprobs - delta[..., None]) * scale).astype(jnp.bfloat16)
    dqueries = jnp.einsum("hqk,khd->qhd", dscores, key_slab, preferred_element_type=jnp.float32)
    dkeys = jnp.einsum("hqk,qhd->khd", dscores, queries, preferred_element_type=jnp.float32)
    return (dqueries, dkeys, dvalues)


MESH = pl.DeviceIdType.MESH
VMEM_LIMIT = 60 * 1024 * 1024
LANES = 128


def ring_place(count):
    me = lax.axis_index("dp")
    core = me % 2
    chip = me // 2
    row, column = chip // 2, chip % 2
    place = (1 - column) * row + column * (count - 1 - row)
    return (core, place)


def chip_at(place, count):
    side = place // (count // 2)
    return (1 - side) * (2 * place) + side * (2 * (count - 1 - place) + 1)


def neighbours(core, place, count):
    right = chip_at((place + 1) % count, count) * 2 + core
    left = chip_at((place + count - 1) % count, count) * 2 + core
    return (right, left, lax.axis_index("dp") + 1 - 2 * core)


def greet(devices):
    barrier = pltpu.get_barrier_semaphore()
    for device in devices:
        pl.semaphore_signal(barrier, inc=1, device_id={"dp": device}, device_id_type=MESH)
    pl.semaphore_wait(barrier, len(devices))


def gather_kernel(
    count, shard_ref, full_ref, own_sem, send_sem, recv_sem, pair_send, pair_recv
):
    rows = shard_ref.shape[0]
    half = rows // 2
    core, place = ring_place(count)
    right, left, partner = neighbours(core, place, count)
    targets = (right, left)

    def piece(way, step):
        shift = count - step if way == 0 else step
        owner = chip_at((place + shift) % count, count) * 2 + core
        return full_ref.at[pl.ds(pl.multiple_of(owner * rows + way * half, half), half)]

    def hop(way, step):
        ref = piece(way, step)
        return pltpu.make_async_remote_copy(
            src_ref=ref,
            dst_ref=ref,
            send_sem=send_sem.at[way, step],
            recv_sem=recv_sem.at[way, step],
            device_id={"dp": targets[way]},
            device_id_type=MESH,
        )

    def share(way, step):
        ref = piece(way, step)
        return pltpu.make_async_remote_copy(
            src_ref=ref,
            dst_ref=ref,
            send_sem=pair_send.at[way, step],
            recv_sem=pair_recv.at[way, step],
            device_id={"dp": partner},
            device_id_type=MESH,
        )

    me = lax.axis_index("dp")
    own = pltpu.make_async_copy(
        shard_ref, full_ref.at[pl.ds(pl.multiple_of(me * rows, rows), rows)], own_sem
    )
    own.start()
    greet((right, left, partner))
    own.wait()
    for way in range(2):
        hop(way, 0).start()
        share(way, 0).start()

    def step_body(step, carry):
        for way in range(2):
            hop(way, step - 1).wait_recv()
            hop(way, step).start()
            share(way, step).start()
        return carry

    lax.fori_loop(1, count - 1, step_body, 0)
    for way in range(2):
        hop(way, count - 2).wait_recv()
        share(way, count - 1).start()

    def drain_hops(step, carry):
        for way in range(2):
            hop(way, step).wait_send()
        return carry

    def drain_shares(step, carry):
        for way in range(2):
            share(way, step).wait_send()
            share(way, step).wait_recv()
        return carry

    lax.fori_loop(0, count - 1, drain_hops, 0)
    lax.fori_loop(0, count, drain_shares, 0)


def ring_gather(shard, devices):
    count = devices // 2
    rows, columns = shard.shape
    return pl.pallas_call(
        functools.partial(gather_kernel, count),
        out_shape=jax.ShapeDtypeStruct((devices * rows, columns), shard.dtype),
        in_specs=[pl.BlockSpec(memory_space=pltpu.VMEM)],
        out_specs=pl.BlockSpec(memory_space=pltpu.HBM),
        scratch_shapes=[
            pltpu.SemaphoreType.DMA,
            pltpu.SemaphoreType.DMA((2, count - 1)),
            pltpu.SemaphoreType.DMA((2, count - 1)),
            pltpu.SemaphoreType.DMA((2, count)),
            pltpu.SemaphoreType.DMA((2, count)),
        ],
        compiler_params=pltpu.CompilerParams(
            collective_id=0, has_side_effects=True, vmem_limit_bytes=8 * 1024 * 1024
        ),
        name="ring_gather",
    )(shard)


def scatter_kernel(count, streams, *refs):
    grads = refs[:streams]
    outs = refs[streams : 2 * streams]
    pairs = refs[2 * streams : 3 * streams]
    sends = refs[3 * streams : 4 * streams]
    recvs = refs[4 * streams : 5 * streams]
    send_sem, recv_sem, pair_send, pair_recv = refs[5 * streams :]
    rows = outs[0].shape[0]
    half = rows // 2
    core, place = ring_place(count)
    right, left, partner = neighbours(core, place, count)
    targets = (right, left)

    def block(way, step, which):
        shift = 2 * count - 1 - step if way == 0 else 1 + step
        owner = chip_at((place + shift) % count, count) * 2 + which
        return pl.ds(pl.multiple_of(owner * rows + way * half, half), half)

    def share(way, step, stream):
        return pltpu.make_async_remote_copy(
            src_ref=grads[stream].at[block(way, step, 1 - core)],
            dst_ref=pairs[stream].at[way, step],
            send_sem=pair_send.at[stream, way, step],
            recv_sem=pair_recv.at[stream, way, step],
            device_id={"dp": partner},
            device_id_type=MESH,
        )

    def hop(way, step, stream):
        return pltpu.make_async_remote_copy(
            src_ref=sends[stream].at[way, step],
            dst_ref=recvs[stream].at[way, step],
            send_sem=send_sem.at[stream, way, step],
            recv_sem=recv_sem.at[stream, way, step],
            device_id={"dp": targets[way]},
            device_id_type=MESH,
        )

    def pair_sum(way, step, stream):
        share(way, step, stream).wait_recv()
        own = grads[stream][block(way, step, core), :].astype(jnp.float32)
        return own + pairs[stream][way, step].astype(jnp.float32)

    greet((right, left, partner))

    def start_shares(step, carry):
        for stream in range(streams):
            for way in range(2):
                share(way, step, stream).start()
        return carry

    lax.fori_loop(0, count, start_shares, 0)
    for stream in range(streams):
        for way in range(2):
            sends[stream][way, 0] = pair_sum(way, 0, stream).astype(jnp.bfloat16)
            hop(way, 0, stream).start()

    def step_body(step, carry):
        for stream in range(streams):
            for way in range(2):
                total = pair_sum(way, step, stream)
                hop(way, step - 1, stream).wait_recv()
                total = total + recvs[stream][way, step - 1].astype(jnp.float32)
                sends[stream][way, step] = total.astype(jnp.bfloat16)
                hop(way, step, stream).start()
        return carry

    lax.fori_loop(1, count - 1, step_body, 0)
    for stream in range(streams):
        for way in range(2):
            total = pair_sum(way, count - 1, stream)
            hop(way, count - 2, stream).wait_recv()
            total = total + recvs[stream][way, count - 2].astype(jnp.float32)
            outs[stream][way * half : (way + 1) * half, :] = total

    def drain_hops(step, carry):
        for stream in range(streams):
            for way in range(2):
                hop(way, step, stream).wait_send()
        return carry

    def drain_shares(step, carry):
        for stream in range(streams):
            for way in range(2):
                share(way, step, stream).wait_send()
        return carry

    lax.fori_loop(0, count - 1, drain_hops, 0)
    lax.fori_loop(0, count, drain_shares, 0)


def ring_scatter(grads, devices):
    count = devices // 2
    streams = len(grads)
    rows = grads[0].shape[0] // devices
    half = rows // 2
    widths = [grad.shape[1] for grad in grads]
    vmem = pl.BlockSpec(memory_space=pltpu.VMEM)
    return pl.pallas_call(
        functools.partial(scatter_kernel, count, streams),
        out_shape=[jax.ShapeDtypeStruct((rows, width), jnp.float32) for width in widths],
        in_specs=[vmem] * streams,
        out_specs=[vmem] * streams,
        scratch_shapes=[pltpu.VMEM((2, count, half, width), jnp.bfloat16) for width in widths]
        + [pltpu.VMEM((2, count - 1, half, width), jnp.bfloat16) for width in widths] * 2
        + [pltpu.SemaphoreType.DMA((streams, 2, count - 1))] * 2
        + [pltpu.SemaphoreType.DMA((streams, 2, count))] * 2,
        compiler_params=pltpu.CompilerParams(
            collective_id=1, has_side_effects=True, vmem_limit_bytes=VMEM_LIMIT
        ),
        name="ring_scatter",
    )(*grads)


def turn(values, cos_table, sin_table, low_half):
    half = HEAD_HALF
    swapped = jnp.where(
        low_half, pltpu.roll(values, LANES - half, 1), pltpu.roll(values, half, 1)
    )
    return values * cos_table + swapped * sin_table


HEAD_HALF = 32


def lane_masks(rows):
    lane = lax.broadcasted_iota(jnp.int32, (rows, LANES), 1)
    return (lane % (2 * HEAD_HALF) < HEAD_HALF, lane < 2 * HEAD_HALF)


def allowed_pairs(pos_col, pos_row, seg_col, seg_row):
    near = jnp.abs(pos_col[...] - pos_row[...]) <= HALO
    return near & (seg_col[...] == seg_row[...])


def head_probs(queries, keys, allowed, scale):
    scores = (
        lax.dot_general(
            queries, keys, (((1,), (1,)), ((), ())), preferred_element_type=jnp.float32
        )
        * scale
    )
    scores = jnp.where(allowed, scores, NEG_FILL)
    top_score = jnp.max(scores, axis=-1, keepdims=True)
    total = jnp.sum(jnp.exp(scores - top_score), axis=-1, keepdims=True)
    return jnp.exp(scores - (top_score + jnp.log(total)))


def attend_kernel(
    scale, width, proj, cos_ref, sin_ref, pos_col, pos_row, seg_col, seg_row, qkv_out, mixed_out
):
    rows = proj.shape[0]
    low_half, first = lane_masks(rows)
    cos_table, sin_table = cos_ref[...], sin_ref[...]
    allowed = allowed_pairs(pos_col, pos_row, seg_col, seg_row)
    for start in range(0, width, LANES):
        queries = turn(proj[:, start : start + LANES], cos_table, sin_table, low_half)
        keys = turn(
            proj[:, width + start : width + start + LANES], cos_table, sin_table, low_half
        ).astype(jnp.bfloat16)
        values = proj[:, 2 * width + start : 2 * width + start + LANES]
        qkv_out[:, start : start + LANES] = queries.astype(jnp.bfloat16)
        qkv_out[:, width + start : width + start + LANES] = keys
        qkv_out[:, 2 * width + start : 2 * width + start + LANES] = values.astype(jnp.bfloat16)
        mixed = jnp.zeros((rows, LANES), jnp.float32)
        for head in range(2):
            mine = first if head == 0 else ~first
            probs = head_probs(
                jnp.where(mine, queries, 0.0).astype(jnp.bfloat16), keys, allowed, scale
            ).astype(jnp.bfloat16)
            mixed = mixed + jnp.dot(
                probs,
                jnp.where(mine, values, 0.0).astype(jnp.bfloat16),
                preferred_element_type=jnp.float32,
            )
        mixed_out[:, start : start + LANES] = mixed.astype(jnp.bfloat16)


def attend_back_kernel(
    scale,
    width,
    qkv,
    mixed_ref,
    dmixed_ref,
    cos_ref,
    sin_ref,
    pos_col,
    pos_row,
    seg_col,
    seg_row,
    dqkv_out,
):
    rows = qkv.shape[0]
    low_half, first = lane_masks(rows)
    cos_table, sin_table = cos_ref[...], -sin_ref[...]
    allowed = allowed_pairs(pos_col, pos_row, seg_col, seg_row)
    over_rows = (((0,), (0,)), ((), ()))
    over_lanes = (((1,), (1,)), ((), ()))
    for start in range(0, width, LANES):
        queries = qkv[:, start : start + LANES].astype(jnp.float32)
        keys = qkv[:, width + start : width + start + LANES]
        keys32 = keys.astype(jnp.float32)
        values = qkv[:, 2 * width + start : 2 * width + start + LANES]
        dmixed = dmixed_ref[:, start : start + LANES].astype(jnp.float32)
        products = dmixed * mixed_ref[:, start : start + LANES].astype(jnp.float32)
        dquery = jnp.zeros((rows, LANES), jnp.float32)
        dkey = jnp.zeros((rows, LANES), jnp.float32)
        dvalue = jnp.zeros((rows, LANES), jnp.float32)
        for head in range(2):
            mine = first if head == 0 else ~first
            head_queries = jnp.where(mine, queries, 0.0).astype(jnp.bfloat16)
            head_keys = jnp.where(mine, keys32, 0.0).astype(jnp.bfloat16)
            head_dmixed = jnp.where(mine, dmixed, 0.0).astype(jnp.bfloat16)
            delta = jnp.sum(jnp.where(mine, products, 0.0), axis=-1, keepdims=True)
            probs = head_probs(head_queries, keys, allowed, scale)
            dprobs = lax.dot_general(
                head_dmixed, values, over_lanes, preferred_element_type=jnp.float32
            )
            dscores = (probs * (dprobs - delta) * scale).astype(jnp.bfloat16)
            dvalue = dvalue + lax.dot_general(
                probs.astype(jnp.bfloat16),
                head_dmixed,
                over_rows,
                preferred_element_type=jnp.float32,
            )
            dkey = dkey + lax.dot_general(
                dscores, head_queries, over_rows, preferred_element_type=jnp.float32
            )
            dquery = dquery + jnp.dot(dscores, head_keys, preferred_element_type=jnp.float32)
        dquery = turn(dquery, cos_table, sin_table, low_half)
        dkey = turn(dkey, cos_table, sin_table, low_half)
        dqkv_out[:, start : start + LANES] = dquery.astype(jnp.bfloat16)
        dqkv_out[:, width + start : width + start + LANES] = dkey.astype(jnp.bfloat16)
        dqkv_out[:, 2 * width + start : 2 * width + start + LANES] = dvalue.astype(jnp.bfloat16)


def local_call(kernel, name, out_shape, operands, flops):
    vmem = pl.BlockSpec(memory_space=pltpu.VMEM)
    single = not isinstance(out_shape, list)
    return pl.pallas_call(
        kernel,
        out_shape=out_shape,
        in_specs=[vmem] * len(operands),
        out_specs=vmem if single else [vmem] * len(out_shape),
        cost_estimate=pl.CostEstimate(
            flops=flops, bytes_accessed=4 * 1024 * 1024, transcendentals=flops // 256
        ),
        compiler_params=pltpu.CompilerParams(vmem_limit_bytes=32 * 1024 * 1024),
        name=name,
    )(*operands)


class PairedAttention:
    def __init__(self, positions, segments, head_size, width):
        rows = positions.shape[0]
        cos_table, sin_table = rotary_tables(positions, head_size)
        cos_table, sin_table = cos_table[:, 0, :], sin_table[:, 0, :]
        self.width = width
        self.scale = 1.0 / math.sqrt(head_size)
        self.flops = 2 * rows * rows * LANES * (width // head_size)
        self.shared = (
            jnp.concatenate([cos_table] * 4, axis=1),
            jnp.concatenate([-sin_table, sin_table] * 2, axis=1),
            positions[:, None],
            positions[None, :],
            segments[:, None],
            segments[None, :],
        )

    def forward(self, projected):
        rows = projected.shape[0]
        self.qkv, self.mixed = local_call(
            functools.partial(attend_kernel, self.scale, self.width),
            "attend",
            [
                jax.ShapeDtypeStruct((rows, 3 * self.width), jnp.bfloat16),
                jax.ShapeDtypeStruct((rows, self.width), jnp.bfloat16),
            ],
            (projected,) + self.shared,
            2 * self.flops,
        )
        return self.mixed

    def backward(self, dmixed):
        rows = dmixed.shape[0]
        return local_call(
            functools.partial(attend_back_kernel, self.scale, self.width),
            "attend_back",
            jax.ShapeDtypeStruct((rows, 3 * self.width), jnp.bfloat16),
            (self.qkv, self.mixed, dmixed) + self.shared,
            5 * self.flops,
        )


class BlockAttention:
    def __init__(self, positions, segments, head_size, width):
        self.total_len = positions.shape[0]
        self.segments = segments
        self.head_size = head_size
        self.width = width
        self.scale = 1.0 / math.sqrt(head_size)
        self.cos_table, self.sin_table = rotary_tables(positions, head_size)

    def heads(self, values):
        return values.reshape(self.total_len, self.width // self.head_size, self.head_size)

    def forward(self, projected):
        width, total_len = self.width, self.total_len
        self.block_rows = min(total_len, 512)
        self.slab_rows = self.block_rows + 2 * HALO
        tables = (self.cos_table, self.sin_table)
        self.queries = rotate(self.heads(projected[:, :width]), *tables).astype(jnp.bfloat16)
        keys = rotate(self.heads(projected[:, width : 2 * width]), *tables).astype(jnp.bfloat16)
        values = self.heads(projected[:, 2 * width :]).astype(jnp.bfloat16)
        pad_spec = ((HALO, HALO), (0, 0), (0, 0))
        self.key_pad = jnp.pad(keys, pad_spec)
        self.value_pad = jnp.pad(values, pad_spec)
        seg_pad = jnp.pad(self.segments, (HALO, HALO), constant_values=-1)
        mixed_parts = []
        self.logsums = []
        self.masks = []
        for start in range(0, total_len, self.block_rows):
            own = slice(start, start + self.block_rows)
            slab = slice(start, start + self.slab_rows)
            allowed = window_mask(
                start + jnp.arange(self.block_rows, dtype=jnp.int32),
                start - HALO + jnp.arange(self.slab_rows, dtype=jnp.int32),
                self.segments[own],
                seg_pad[slab],
                HALO,
                total_len,
            )
            mixed, logsum = attend_block(
                self.queries[own], self.key_pad[slab], self.value_pad[slab], allowed, self.scale
            )
            self.masks.append(allowed)
            self.logsums.append(logsum)
            mixed_parts.append(mixed)
        self.mixed = jnp.concatenate(mixed_parts, axis=0).astype(jnp.bfloat16)
        return self.mixed.reshape(total_len, width)

    def backward(self, dmixed):
        total_len = self.total_len
        dmixed = self.heads(dmixed)
        padded = (total_len + 2 * HALO,) + dmixed.shape[1:]
        dkey_pad = jnp.zeros(padded, jnp.float32)
        dvalue_pad = jnp.zeros(padded, jnp.float32)
        dquery_parts = []
        for index, start in enumerate(range(0, total_len, self.block_rows)):
            own = slice(start, start + self.block_rows)
            slab = slice(start, start + self.slab_rows)
            dqueries, dkeys, dvalues = attend_back(
                self.queries[own],
                self.key_pad[slab],
                self.value_pad[slab],
                self.masks[index],
                self.scale,
                self.logsums[index],
                self.mixed[own],
                dmixed[own],
            )
            dquery_parts.append(dqueries)
            dkey_pad = dkey_pad.at[slab].add(dkeys)
            dvalue_pad = dvalue_pad.at[slab].add(dvalues)
        inner = slice(HALO, HALO + total_len)
        tables = (self.cos_table, self.sin_table)
        parts = [
            unrotate(jnp.concatenate(dquery_parts, axis=0), *tables),
            unrotate(dkey_pad[inner], *tables),
            dvalue_pad[inner],
        ]
        return jnp.concatenate(
            [part.reshape(total_len, self.width) for part in parts], axis=1
        ).astype(jnp.bfloat16)


def dot(left, right, left_dim, right_dim):
    return lax.dot_general(
        left,
        right,
        (((left_dim,), (right_dim,)), ((), ())),
        preferred_element_type=jnp.float32,
    )


def padded_to_lanes(values):
    return jnp.pad(values, ((0, 0), (0, -values.shape[1] % LANES)))


def high_and_low(gain):
    high = gain.astype(jnp.bfloat16)
    return [high[:, None], (gain - high.astype(jnp.float32)).astype(jnp.bfloat16)[:, None]]


def per_device(
    devices,
    seq_size,
    tokens,
    segments,
    cotangent,
    qkv_weight,
    out_weight,
    in_weight,
    down_weight,
    attn_gain,
    mlp_gain,
):
    layer_in = tokens[0]
    seg_local = segments[0]
    cot_local = cotangent[0]
    own_rows, model_width = layer_in.shape
    head_size = model_width // HEADS
    local_width = qkv_weight.shape[2]
    local_hidden = in_weight.shape[2]
    shard_rows = qkv_weight.shape[0]
    total_len = own_rows * seq_size
    paired = (
        seq_size == 2
        and total_len <= 512
        and local_width % LANES == 0
        and head_size == 2 * HEAD_HALF
    )
    swap = [(0, 1), (1, 0)]

    def rows_of_all(values):
        if paired:
            return jnp.concatenate([values, lax.ppermute(values, "seq", swap)], axis=0)
        return lax.all_gather(values, "seq", axis=0, tiled=True)

    def sum_to_owner(partial):
        if paired:
            other = lax.ppermute(partial[own_rows:].astype(jnp.bfloat16), "seq", swap)
            return partial[:own_rows] + other.astype(jnp.float32)
        return lax.psum_scatter(
            partial.astype(jnp.bfloat16), "seq", scatter_dimension=0, tiled=True
        ).astype(jnp.float32)

    def sum_over_seq(part):
        if paired:
            return part + lax.ppermute(part, "seq", swap)
        return lax.psum(part, "seq")

    first_pack = jnp.concatenate(
        [qkv_weight.reshape(shard_rows, 3 * local_width), out_weight.T]
        + [
            padded_to_lanes(
                jnp.concatenate(high_and_low(attn_gain) + high_and_low(mlp_gain), axis=1)
            )
        ],
        axis=1,
    )
    second_pack = jnp.concatenate(
        [
            padded_to_lanes(in_weight[:, 0, :]),
            padded_to_lanes(in_weight[:, 1, :]),
            padded_to_lanes(down_weight.T),
        ],
        axis=1,
    )
    wide = second_pack.shape[1] // 3
    first_full = ring_gather(first_pack, devices)
    second_full = lax.all_gather(second_pack, "dp", axis=0, tiled=True)
    full_qkv = first_full[:, : 3 * local_width]
    full_out = first_full[:, 3 * local_width : 4 * local_width]
    gains = first_full[:, 4 * local_width : 4 * local_width + 4].astype(jnp.float32)
    gain_attn = gains[:, 0] + gains[:, 1]
    gain_mlp = gains[:, 2] + gains[:, 3]
    full_in = second_full[:, : 2 * wide]
    full_down = second_full[:, 2 * wide :]

    inputs32 = layer_in.astype(jnp.float32)
    normed_one, unit_one, inv_one = norm_forward(inputs32, gain_attn)
    normed_full = rows_of_all(normed_one.astype(jnp.bfloat16))
    cot_full = rows_of_all(cot_local)
    if paired:
        seg_full = rows_of_all(
            jnp.broadcast_to(seg_local.astype(jnp.float32)[:, None], (own_rows, LANES))
        )[:, 0].astype(jnp.int32)
        place = lax.axis_index("seq")
        arange = jnp.arange(own_rows, dtype=jnp.int32)
        positions = jnp.concatenate(
            [place * own_rows + arange, (1 - place) * own_rows + arange], axis=0
        )
        attention = PairedAttention(positions, seg_full, head_size, local_width)
    else:
        seg_full = rows_of_all(seg_local.astype(jnp.bfloat16)).astype(jnp.int32)
        positions = jnp.arange(total_len, dtype=jnp.int32)
        attention = BlockAttention(positions, seg_full, head_size, local_width)

    mixed = attention.forward(dot(normed_full, full_qkv, 1, 0))
    residual = inputs32 + sum_to_owner(dot(mixed, full_out, 1, 1))
    normed_two, unit_two, inv_two = norm_forward(residual, gain_mlp)
    normed_two_full = rows_of_all(normed_two.astype(jnp.bfloat16))
    expanded = dot(normed_two_full, full_in, 1, 0)
    gate_in = expanded[:, :wide]
    linear_in = expanded[:, wide:]
    activated = gelu_value(gate_in)
    middle_b = (activated * linear_in).astype(jnp.bfloat16)
    layer_out = (residual + sum_to_owner(dot(middle_b, full_down, 1, 1))).astype(jnp.bfloat16)

    down_grad = dot(cot_full, middle_b, 0, 0).astype(jnp.bfloat16)
    down_share = lax.psum_scatter(down_grad, "dp", scatter_dimension=0, tiled=True)
    dmiddle = dot(cot_full, full_down, 1, 0)
    dexpanded_b = jnp.concatenate(
        [dmiddle * linear_in * gelu_slope(gate_in), dmiddle * activated], axis=1
    ).astype(jnp.bfloat16)
    dnormed_two = sum_to_owner(dot(dexpanded_b, full_in, 1, 1))
    in_grad = dot(normed_two_full, dexpanded_b, 0, 0).astype(jnp.bfloat16)
    dres_norm, mlp_gain_part = norm_backward(dnormed_two, gain_mlp, unit_two, inv_two)
    dresidual = cot_local.astype(jnp.float32) + dres_norm
    dres_full = rows_of_all(dresidual.astype(jnp.bfloat16))
    dmixed = dot(dres_full, full_out, 1, 0).astype(jnp.bfloat16)
    out_grad = dot(dres_full, mixed, 0, 0).astype(jnp.bfloat16)
    dqkv_b = attention.backward(dmixed)
    dnormed_one = sum_to_owner(dot(dqkv_b, full_qkv, 1, 1))
    qkv_grad = dot(normed_full, dqkv_b, 0, 0).astype(jnp.bfloat16)
    dinput_norm, attn_gain_part = norm_backward(dnormed_one, gain_attn, unit_one, inv_one)
    tokens_grad = (dresidual + dinput_norm).astype(jnp.bfloat16)
    gain_sums = sum_over_seq(jnp.stack([attn_gain_part, mlp_gain_part]))
    gain_grad = padded_to_lanes(gain_sums.T).astype(jnp.bfloat16)

    in_share, qkv_share, out_share, gain_share = ring_scatter(
        [in_grad, qkv_grad, out_grad, gain_grad], devices
    )
    return (
        layer_out[None],
        tokens_grad[None],
        qkv_share.reshape(shard_rows, 3, local_width),
        out_share.T,
        jnp.stack([in_share[:, :local_hidden], in_share[:, wide : wide + local_hidden]], axis=1),
        down_share.astype(jnp.float32)[:, :local_hidden].T,
        gain_share[:, 0],
        gain_share[:, 1],
    )


def solution(mesh):
    return jax.shard_map(
        functools.partial(per_device, mesh.shape["dp"], mesh.shape["seq"]),
        mesh=mesh,
        in_specs=(
            P("dp", "seq", None),
            P("dp", "seq"),
            P("dp", "seq", None),
            P("dp", None, "seq"),
            P("seq", "dp"),
            P("dp", None, "seq"),
            P("seq", "dp"),
            P("dp"),
            P("dp"),
        ),
        out_specs=(
            P("dp", "seq", None),
            P("dp", "seq", None),
            P("dp", None, "seq"),
            P("seq", "dp"),
            P("dp", None, "seq"),
            P("seq", "dp"),
            P("dp"),
            P("dp"),
        ),
        check_vma=False,
    )
```

time: 640 us -> 240 us (0.38)
  waiting for transfers between devices: 373 us -> 30.1 us
  Pallas kernels: 0 us -> 133 us
  blocking collectives: 116 us -> 0 us
  local copies, waits for them, and re-layouts: 59.6 us -> 13.3 us
  matrix products: 44.6 us -> 25.7 us
  other arithmetic: 28.3 us -> 11.3 us
  starting transfers between devices: 0.66 us -> 11.1 us
    unnamed x12 -> x2, waiting for transfers between devices: 197 us -> 0.03 us
    pallas_call x0 -> x4, Pallas kernels: none -> 133 us  [the longest x1 71.3 us: ring_scatter(): pl.pallas_call(functools.partial(scatter_kernel, count, streams), out_sha...]
    reduce_scatter x6 -> x1, waiting for transfers between devices: 91 us -> 0.01 us  [per_device(): lax.psum_scatter(down_grad, 'dp', scatter_dimension=0, tiled=True)]
    all_gather x4 -> x1, waiting for transfers between devices: 84.6 us -> 0.01 us  [per_device(): second_full = lax.all_gather(second_pack, 'dp', axis=0, tiled=True)]
    unnamed x2 -> x0, blocking collectives: 64.6 us -> none
    all_gather x5 -> x0, blocking collectives: 46 us -> none  [the longest x1 16 us: per_device(): lax.all_gather(cot_local, 'seq', axis=0, tiled=True)]
    ppermute x0 -> x10, waiting for transfers between devices: none -> 30.1 us  [the longest x5 15.5 us: rows_of_all(): return jnp.concatenate([values, lax.ppermute(values, 'seq', swap)], axis=0)]
    convert_element_type x4 -> x0, local copies, waits for them, and re-layouts: 27.3 us -> none  [the longest x1 15 us: per_device(): in_grad.astype(jnp.bfloat16)]
  transfers between devices with their start and end apart: 11 -> 12, of which waited for: 8 -> 8; matrix products, arithmetic and copies ran while one was open for 15% -> 15% of each run, Pallas kernels for 0% -> 56%
where the time goes in v1:
time: 240 us
  Pallas kernels  133 us (55%)
  waiting for transfers between devices  30.1 us (13%)
  matrix products  25.7 us (11%)
  between operations  14.6 us (6%)
  local copies, waits for them, and re-layouts  13.3 us (6%)
  other arithmetic  11.3 us (5%)
  starting transfers between devices  11.1 us (5%)
    pallas_call x1, Pallas kernels, ring_scatter(): pl.pallas_call(functools.partial(scatter_kernel, count, streams), out_sha...  71.3 us
    pallas_call x1, Pallas kernels, ring_gather(): pl.pallas_call(functools.partial(gather_kernel, count), out_shape=jax.Sha...  56.4 us
    dot_general x12, matrix products, dot(): lax.dot_general(left, right, (((left_dim,), (right_dim,)), ((), ())), pre...  25.7 us
    ppermute x5, waiting for transfers between devices, rows_of_all(): return jnp.concatenate([values, lax.ppermute(values, 'seq', swap)], axis=0)  15.5 us
    ppermute x4, waiting for transfers between devices, sum_to_owner(): other = lax.ppermute(partial[own_rows:].astype(jnp.bfloat16), 'seq', swap)  13.1 us
    ppermute x5, starting transfers between devices, rows_of_all(): return jnp.concatenate([values, lax.ppermute(values, 'seq', swap)], axis=0)  6.3 us
    pallas_call x2, Pallas kernels, local_call(): pl.pallas_call(kernel, out_shape=out_shape, in_specs=[vmem] * len(operand...  5.7 us
    unnamed x60, local copies, waits for them, and re-layouts  4.94 us
  transfers between devices with their start and end apart: 12, of which 8 were waited for; matrix products, arithmetic and copies ran while one was open for 15% of the time, Pallas kernels for 56%

profile of v1, /device:TPU:0, one launch (start us, length us, event | category | flops | bytes accessed | tf_op | source)
XLA Modules:
  0.0 239.6 jit_solution(4000006857791246161)
XLA Ops:
  7.3 1.8 fusion.67
  9.1 1.8 fusion.35
  11.1 3.0 %collective-permute-start.1 = (f32[128,128]{1,0:T(8,128)S(1)}, f32[128,128]{1,0:T(8,128)S(1)}, u32[]{:S(2)}, u32[]{:S(2)}) collective-permute-start(f32[128,128]{1,0:T(8,128)S(1)} %broadcast_in_dim.24), channel_id=1, source_target_pairs={{0,1},{1,0},{2,3},{3,2},{4,5},{5,4},{6,7},{7,6},{8,9},{9,8},{10,11... | collective-permute-start | bytes 196616 | tf_op jit(solution)/shard_map/ppermute | solution.py:673
  14.3 56.4 %ring_gather.1 = bf16[1024,2176]{1,0:T(8,128)(2,1)S(1)} custom-call(bf16[64,2176]{1,0:T(8,128)(2,1)S(1)} %fusion.48.shard_ref), custom_call_target="tpu_custom_call" | custom-call | tf_op jit(solution)/shard_map/ring_gather/pallas_call | solution.py:228
  71.1 1.8 copy-done
  75.3 7.3 %collective-permute-done = bf16[128,1024]{1,0:T(8,128)(2,1)S(1)} collective-permute-done((bf16[128,1024]{1,0:T(8,128)(2,1)S(1)}, bf16[128,1024]{1,0:T(8,128)(2,1)S(1)}, u32[]{:S(2)}, u32[]{:S(2)}) %collective-permute-start) | collective-permute-done | bytes 262176 | tf_op jit(solution)/shard_map/ppermute | solution.py:673
  82.6 3.0 %fusion.6.proj = f32[256,1536]{1,0:T(8,128)S(1)} fusion(bf16[1024,2176]{1,0:T(8,128)(2,1)} %copy-done, bf16[128,1024]{1,0:T(8,128)(2,1)S(1)} %collective-permute-done, bf16[128,1024]{1,0:T(8,128)(2,1)S(1)} %fusion.36), kind=kOutput, calls=%fused_computation.9 | convolution fusion | flops 806354944 | bytes 5242880 | tf_op jit(solution)/shard_map/dot_general | solution.py:624
  85.6 2.5 %attend.1 = (bf16[256,1536]{1,0:T(8,128)(2,1)S(1)}, bf16[256,512]{1,0:T(8,128)(2,1)S(1)}) custom-call(f32[256,1536]{1,0:T(8,128)S(1)} %fusion.6.proj, f32[256,128]{1,0:T(8,128)S(1)} %pad_maximum_fusion.17.cos_ref, f32[256,128]{1,0:T(8,128)S(1)} %pad_maximum_fusion.18.sin_ref, s32[256,1]{1,0:T(8,128)S(1)} %copy.52.pos_col, s32[1,256]{1,0:T(1,128)S(1)} %bitcast.88, ...), custom_call_target="tpu_custom_call" | custom-call | flops 268435456 | bytes 4194304 | tf_op jit(solution)/shard_map/attend/pallas_call | solution.py:486
  88.1 1.7 fusion.23
  90.2 7.5 %collective-permute-done.2 = bf16[128,1024]{1,0:T(8,128)(2,1)S(1)} collective-permute-done((bf16[128,1024]{1,0:T(8,128)(2,1)S(1)}, bf16[128,1024]{1,0:T(8,128)(2,1)S(1)}, u32[]{:S(2)}, u32[]{:S(2)}) %collective-permute-start.2) | collective-permute-done | bytes 262176 | tf_op jit(solution)/shard_map/ppermute | solution.py:678
  98.9 1.5 collective-permute-start.5
  100.4 7.1 %collective-permute-done.3 = bf16[128,1024]{1,0:T(8,128)(2,1)S(1)} collective-permute-done((bf16[128,1024]{1,0:T(8,128)(2,1)S(1)}, bf16[128,1024]{1,0:T(8,128)(2,1)S(1)}, u32[]{:S(2)}, u32[]{:S(2)}) %collective-permute-start.3) | collective-permute-done | bytes 262176 | tf_op jit(solution)/shard_map/ppermute | solution.py:673
  107.5 4.5 %fusion.2 = f32[256,2816]{1,0:T(8,128)S(1)} fusion(bf16[1024,4224]{1,0:T(8,128)(2,1)} %all-gather.2.cloned.1.call-done, bf16[128,1024]{1,0:T(8,128)(2,1)S(1)} %collective-permute-done.3, bf16[128,1024]{1,0:T(8,128)(2,1)S(1)} %multiply_convert_fusion.2), kind=kOutput, calls=%fused_computation.3 | convolution fusion | flops 1477443584 | bytes 9175040 | tf_op jit(solution)/shard_map/dot_general | solution.py:624
  112.8 1.5 fusion.17
  116.4 1.7 fusion
  119.4 1.5 collective-permute-start.4
  120.8 2.6 %convolution_convert_fusion.1 = bf16[1024,1408]{1,0:T(8,128)(2,1)} fusion(bf16[256,1408]{1,0:T(8,128)(2,1)S(1)} %get-tuple-element.68, bf16[128,1024]{1,0:T(8,128)(2,1)S(1)} %copy-done.16, bf16[128,1024]{1,0:T(8,128)(2,1)S(1)} %bitcast.94), kind=kOutput, calls=%fused_computation.5 | convolution fusion | flops 740687872 | bytes 4128768 | tf_op jit(solution)/shard_map/dot_general | solution.py:624
  123.5 2.9 %collective-permute-done.6 = bf16[128,1024]{1,0:T(8,128)(2,1)} collective-permute-done((bf16[128,1024]{1,0:T(8,128)(2,1)}, bf16[128,1024]{1,0:T(8,128)(2,1)}, u32[]{:S(2)}, u32[]{:S(2)}) %collective-permute-start.6) | collective-permute-done | bytes 262176 | tf_op jit(solution)/shard_map/ppermute | solution.py:678
  126.4 1.2 multiply_reduce_fusion
  127.6 1.6 collective-permute-done.4
  129.2 2.2 fusion.64
  132.6 4.2 %convolution_convert_fusion.refs_0_ = bf16[1024,2816]{1,0:T(8,128)(2,1)} fusion(bf16[256,1408]{1,0:T(8,128)(2,1)S(1)} %copy-done.11, bf16[256,1408]{1,0:T(8,128)(2,1)S(1)} %copy-done.9, bf16[128,1024]{1,0:T(8,128)(2,1)S(1)} %copy-done.14, bf16[128,1024]{1,0:T(8,128)(2,1)S(1)} %copy-done.5), kind=kOutput, calls=%fused_computation | convolution fusion | flops 1483210752 | bytes 7733248 | tf_op jit(solution)/shard_map/dot_general | solution.py:624
  138.3 3.2 %attend_back.1 = bf16[256,1536]{1,0:T(8,128)(2,1)S(1)} custom-call(bf16[256,1536]{1,0:T(8,128)(2,1)S(1)} %get-tuple-element.15.qkv, bf16[256,512]{1,0:T(8,128)(2,1)S(1)} %get-tuple-element.14.mixed_ref, bf16[256,512]{1,0:T(8,128)(2,1)S(1)} %convolution_convert_fusion.4.dmixed_ref, f32[256,128]{1,0:T(8,128)S(1)} %pad_maximum_fusion.17.cos_ref, ...), custom_call_target="tpu_custom_call" | custom-call | flops 671088640 | bytes 4194304 | tf_op jit(solution)/shard_map/attend_back/pallas_call | solution.py:486
  142.6 1.2 collective-permute-start.8
  143.8 2.7 %convolution_convert_fusion.2.refs_1_ = bf16[1024,1536]{1,0:T(8,128)(2,1)} fusion(bf16[256,1536]{1,0:T(8,128)(2,1)S(1)} %attend_back.1, bf16[128,1024]{1,0:T(8,128)(2,1)S(1)} %copy-done.18, bf16[128,1024]{1,0:T(8,128)(2,1)S(1)} %copy-done.7), kind=kOutput, calls=%fused_computation.6 | convolution fusion | flops 807927808 | bytes 4456448 | tf_op jit(solution)/shard_map/dot_general | solution.py:624
  146.5 1.4 convolution_convert_fusion.3.refs_2_
  149.3 1.2 collective-permute-start.9
  151.5 1.5 collective-permute-done.9
  154.0 71.3 %ring_scatter.1 = (f32[64,2816]{1,0:T(8,128)}, f32[64,1536]{1,0:T(8,128)}, f32[64,512]{1,0:T(8,128)}, f32[64,128]{1,0:T(8,128)}) custom-call(bf16[1024,2816]{1,0:T(8,128)(2,1)} %convolution_convert_fusion.refs_0_, bf16[1024,1536]{1,0:T(8,128)(2,1)} %convolution_convert_fusion.2.refs_1_, bf16[1024,512]{1,0:T(8,128)(2,1)} %convolution_convert_fusion.3.refs_2_, ...), custom_call_target="tpu_custom_call" | custom-call | tf_op jit(solution)/shard_map/ring_scatter/pallas_call | solution.py:345
  225.3 1.8 copy.66
  228.3 1.4 copy.58
  230.4 1.7 convert_bitcast_fusion.1
  (123 shorter events, 18.3 us)
Async XLA Ops:
  7.2 6.9 %copy-start.23 = (f32[64]{0:T(128)S(1)}, f32[64]{0:T(128)}, u32[]{:S(2)}) copy-start(f32[64]{0:T(128)} %param.17) | copy-start | bytes 772
  7.2 6.9 %copy-start.24 = (f32[64]{0:T(128)S(1)}, f32[64]{0:T(128)}, u32[]{:S(2)}) copy-start(f32[64]{0:T(128)} %param.16) | copy-start | bytes 772
  7.2 7.1 %copy-start.19 = (bf16[64,3,512]{2,0,1:T(8,128)(2,1)S(1)}, bf16[64,3,512]{2,0,1:T(8,128)(2,1)}, u32[]{:S(2)}) copy-start(bf16[64,3,512]{2,0,1:T(8,128)(2,1)} %param.12) | copy-start | bytes 589828
  7.2 7.1 %copy-start.22 = (bf16[512,64]{0,1:T(8,128)(2,1)S(1)}, bf16[512,64]{0,1:T(8,128)(2,1)}, u32[]{:S(2)}) copy-start(bf16[512,64]{0,1:T(8,128)(2,1)} %param.13) | copy-start | bytes 196612
  7.2 100.3 %all-gather.2.cloned.1.call-start = ((), (), s32[]{:S(2)}) async-start(), calls=%async_computation.1 | async-start | bytes 9191424 | tf_op jit(solution)/shard_map/all_gather | solution.py:708
  10.9 219.5 %reduce-scatter.2.cloned.1.call-start = ((), (), s32[]{:S(2)}) async-start(), calls=%async_computation.2 | async-start | bytes 3063808 | tf_op jit(solution)/shard_map/reduce_scatter | solution.py:748
  11.0 59.8 %copy-start.1 = (bf16[1,128,1024]{2,1,0:T(8,128)(2,1)S(1)}, bf16[1,128,1024]{2,1,0:T(8,128)(2,1)}, u32[]{:S(2)}) copy-start(bf16[1,128,1024]{2,1,0:T(8,128)(2,1)} %param.9) | copy-start | bytes 786436
  11.1 64.1 %collective-permute-start.1 = (f32[128,128]{1,0:T(8,128)S(1)}, f32[128,128]{1,0:T(8,128)S(1)}, u32[]{:S(2)}, u32[]{:S(2)}) collective-permute-start(f32[128,128]{1,0:T(8,128)S(1)} %broadcast_in_dim.24), channel_id=1, source_target_pairs={{0,1},{1,0},{2,3},{3,2},{4,5},{5,4},{6,7},{7,6},{8,9},{9,8},{10,11... | collective-permute-start | bytes 196616 | tf_op jit(solution)/shard_map/ppermute | solution.py:673
  74.0 11.6 %copy-start.6 = (bf16[128,1024]{1,0:T(8,128)(2,1)}, bf16[128,1024]{1,0:T(8,128)(2,1)S(1)}, u32[]{:S(2)}) copy-start(bf16[128,1024]{1,0:T(8,128)(2,1)S(1)} %fusion.36) | copy-start | bytes 786436
  74.0 8.6 %collective-permute-start = (bf16[128,1024]{1,0:T(8,128)(2,1)S(1)}, bf16[128,1024]{1,0:T(8,128)(2,1)S(1)}, u32[]{:S(2)}, u32[]{:S(2)}) collective-permute-start(bf16[128,1024]{1,0:T(8,128)(2,1)S(1)} %fusion.36), channel_id=1, source_target_pairs={{0,1},{1,0},{2,3},{3,2},{4,5},{5,4},{6,7},{7,6},{8,9},{9,8},{10,11... | collective-permute-start | bytes 786440 | tf_op jit(solution)/shard_map/ppermute | solution.py:673
  88.1 10.9 %copy-start.2 = (bf16[1,128,1024]{2,1,0:T(8,128)(2,1)S(1)}, bf16[1,128,1024]{2,1,0:T(8,128)(2,1)}, u32[]{:S(2)}) copy-start(bf16[1,128,1024]{2,1,0:T(8,128)(2,1)} %param.11) | copy-start | bytes 786436
  89.9 7.9 %collective-permute-start.2 = (bf16[128,1024]{1,0:T(8,128)(2,1)S(1)}, bf16[128,1024]{1,0:T(8,128)(2,1)S(1)}, u32[]{:S(2)}, u32[]{:S(2)}) collective-permute-start(bf16[128,1024]{1,0:T(8,128)(2,1)S(1)} %slice.210), channel_id=1, source_target_pairs={{0,1},{1,0},{2,3},{3,2},{4,5},{5,4},{6,7},{7,6},{8,9},{9,8},{10,11... | collective-permute-start | bytes 786440 | tf_op jit(solution)/shard_map/ppermute | solution.py:678
  98.3 13.7 %copy-start.4 = (bf16[128,1024]{1,0:T(8,128)(2,1)}, bf16[128,1024]{1,0:T(8,128)(2,1)S(1)}, u32[]{:S(2)}) copy-start(bf16[128,1024]{1,0:T(8,128)(2,1)S(1)} %multiply_convert_fusion.2) | copy-start | bytes 786436
  98.3 9.2 %collective-permute-start.3 = (bf16[128,1024]{1,0:T(8,128)(2,1)S(1)}, bf16[128,1024]{1,0:T(8,128)(2,1)S(1)}, u32[]{:S(2)}, u32[]{:S(2)}) collective-permute-start(bf16[128,1024]{1,0:T(8,128)(2,1)S(1)} %multiply_convert_fusion.2), channel_id=1, source_target_pairs={{0,1},{1,0},{2,3},{3,2},{4,5},{5,4},{6,7},{7,6},{8,9},{9,8},{10,11... | collective-permute-start | bytes 786440 | tf_op jit(solution)/shard_map/ppermute | solution.py:673
  98.9 13.1 %collective-permute-start.5 = (bf16[128,1024]{1,0:T(8,128)(2,1)S(1)}, bf16[128,1024]{1,0:T(8,128)(2,1)S(1)}, u32[]{:S(2)}, u32[]{:S(2)}) collective-permute-start(bf16[128,1024]{1,0:T(8,128)(2,1)S(1)} %bitcast.92), channel_id=1, source_target_pairs={{0,1},{1,0},{2,3},{3,2},{4,5},{5,4},{6,7},{7,6},{8,9},{9,8},{10,11... | collective-permute-start | bytes 786440 | tf_op jit(solution)/shard_map/ppermute | solution.py:673
  107.5 4.5 %copy-start.13 = (bf16[128,1024]{1,0:T(8,128)(2,1)}, bf16[128,1024]{1,0:T(8,128)(2,1)S(1)}, u32[]{:S(2)}) copy-start(bf16[128,1024]{1,0:T(8,128)(2,1)S(1)} %collective-permute-done.3) | copy-start | bytes 786436
  107.5 5.2 %copy-start.25 = (bf16[1024,4224]{1,0:T(8,128)(2,1)S(1)}, bf16[1024,4224]{1,0:T(8,128)(2,1)}, u32[]{:S(2)}) copy-start(bf16[1024,4224]{1,0:T(8,128)(2,1)} %all-gather.2.cloned.1.call-done) | copy-start | bytes 25952260
  116.4 4.5 %copy-start.3 = (bf16[1,128,1024]{2,1,0:T(8,128)(2,1)S(1)}, bf16[1,128,1024]{2,1,0:T(8,128)(2,1)}, u32[]{:S(2)}) copy-start(bf16[1,128,1024]{2,1,0:T(8,128)(2,1)} %param.11) | copy-start | bytes 786436
  116.4 4.5 %copy-start.16 = (bf16[128,1024]{1,0:T(8,128)(2,1)S(1)}, bf16[128,1024]{1,0:T(8,128)(2,1)}, u32[]{:S(2)}) copy-start(bf16[128,1024]{1,0:T(8,128)(2,1)} %copy-done.15) | copy-start | bytes 786436
  118.8 7.6 %collective-permute-start.6 = (bf16[128,1024]{1,0:T(8,128)(2,1)}, bf16[128,1024]{1,0:T(8,128)(2,1)}, u32[]{:S(2)}, u32[]{:S(2)}) collective-permute-start(bf16[128,1024]{1,0:T(8,128)(2,1)} %slice.208), channel_id=1, source_target_pairs={{0,1},{1,0},{2,3},{3,2},{4,5},{5,4},{6,7},{7,6},{8,9},{9,8},{10,11... | collective-permute-start | bytes 786440 | tf_op jit(solution)/shard_map/ppermute | solution.py:678
  119.4 9.8 %collective-permute-start.4 = (bf16[128,1024]{1,0:T(8,128)(2,1)}, bf16[128,1024]{1,0:T(8,128)(2,1)}, u32[]{:S(2)}, u32[]{:S(2)}) collective-permute-start(bf16[128,1024]{1,0:T(8,128)(2,1)} %slice.209), channel_id=1, source_target_pairs={{0,1},{1,0},{2,3},{3,2},{4,5},{5,4},{6,7},{7,6},{8,9},{9,8},{10,11... | collective-permute-start | bytes 786440 | tf_op jit(solution)/shard_map/ppermute | solution.py:678
  123.4 9.1 %copy-start.5 = (bf16[128,1024]{1,0:T(8,128)(2,1)S(1)}, bf16[128,1024]{1,0:T(8,128)(2,1)}, u32[]{:S(2)}) copy-start(bf16[128,1024]{1,0:T(8,128)(2,1)} %copy-done.4) | copy-start | bytes 786436
  123.5 9.1 %copy-start.9 = (bf16[256,1408]{1,0:T(8,128)(2,1)S(1)}, bf16[256,1408]{1,0:T(8,128)(2,1)}, u32[]{:S(2)}) copy-start(bf16[256,1408]{1,0:T(8,128)(2,1)} %copy-done.8) | copy-start | bytes 2162692
  123.5 9.1 %copy-start.11 = (bf16[256,1408]{1,0:T(8,128)(2,1)S(1)}, bf16[256,1408]{1,0:T(8,128)(2,1)}, u32[]{:S(2)}) copy-start(bf16[256,1408]{1,0:T(8,128)(2,1)} %copy-done.10) | copy-start | bytes 2162692
  123.5 9.1 %copy-start.14 = (bf16[128,1024]{1,0:T(8,128)(2,1)S(1)}, bf16[128,1024]{1,0:T(8,128)(2,1)}, u32[]{:S(2)}) copy-start(bf16[128,1024]{1,0:T(8,128)(2,1)} %copy-done.13) | copy-start | bytes 786436
  131.4 6.4 %slice-start = ((s8[4456448]{0:T(1024)(128)(4,1)}), s8[4194304]{0:T(1024)(128)(4,1)S(1)}, s32[]{:S(2)}) async-start(s8[4456448]{0:T(1024)(128)(4,1)} %bitcast.85), calls=%async_computation.3 | async-start | bytes 8388608
  131.5 6.4 %slice-start.1 = ((s8[4456448]{0:T(1024)(128)(4,1)}), s8[262144]{0:T(1024)(128)(4,1)S(1)}, s32[]{:S(2)}) async-start(s8[4456448]{0:T(1024)(128)(4,1)} %bitcast.85), calls=%async_computation.4 | async-start | bytes 524288
  131.5 6.4 %collective-permute-start.7 = (bf16[128,1024]{1,0:T(8,128)(2,1)S(1)}, bf16[128,1024]{1,0:T(8,128)(2,1)S(1)}, u32[]{:S(2)}, u32[]{:S(2)}) collective-permute-start(bf16[128,1024]{1,0:T(8,128)(2,1)S(1)} %get-tuple-element.62), channel_id=1, source_target_pairs={{0,1},{1,0},{2,3},{3,2},{4,5},{5,4},{6,7},{7,6},{8,9},{9,8},{10,11... | collective-permute-start | bytes 786440 | tf_op jit(solution)/shard_map/ppermute | solution.py:673
  142.6 6.4 %collective-permute-start.8 = (bf16[128,1024]{1,0:T(8,128)(2,1)S(1)}, bf16[128,1024]{1,0:T(8,128)(2,1)S(1)}, u32[]{:S(2)}, u32[]{:S(2)}) collective-permute-start(bf16[128,1024]{1,0:T(8,128)(2,1)S(1)} %slice.207), channel_id=1, source_target_pairs={{0,1},{1,0},{2,3},{3,2},{4,5},{5,4},{6,7},{7,6},{8,9},{9,8},{10,11... | collective-permute-start | bytes 786440 | tf_op jit(solution)/shard_map/ppermute | solution.py:678
  149.3 3.7 %collective-permute-start.9 = (f32[2,1024]{1,0:T(2,128)S(1)}, f32[2,1024]{1,0:T(2,128)S(1)}, u32[]{:S(2)}, u32[]{:S(2)}) collective-permute-start(f32[2,1024]{1,0:T(2,128)S(1)} %pad_maximum_fusion.19), channel_id=1, source_target_pairs={{0,1},{1,0},{2,3},{3,2},{4,5},{5,4},{6,7},{7,6},{8,9},{9,8},{10,11... | collective-permute-start | bytes 24584 | tf_op jit(solution)/shard_map/ppermute | solution.py:686
  225.3 4.4 %copy-start.21 = (f32[64,128]{1,0:T(8,128)S(1)}, f32[64,128]{1,0:T(8,128)}, u32[]{:S(2)}) copy-start(f32[64,128]{1,0:T(8,128)} %get-tuple-element.19) | copy-start | bytes 98308
  225.3 6.8 %copy-start.20 = (f32[64,512]{1,0:T(8,128)S(1)}, f32[64,512]{1,0:T(8,128)}, u32[]{:S(2)}) copy-start(f32[64,512]{1,0:T(8,128)} %get-tuple-element.17) | copy-start | bytes 393220
  (9 other events, 20.1 us)
Sparse Core Ops, SparseCore 0:
  11.0 88.3 all-gather.1
  123.6 72.2 reduce-scatter.1

commit v2 on v1

--- a/solution.py
+++ b/solution.py
@@ -148,100 +148,112 @@
     pl.semaphore_wait(barrier, len(devices))
 
 
-def gather_kernel(
-    count, shard_ref, full_ref, own_sem, send_sem, recv_sem, pair_send, pair_recv
-):
-    rows = shard_ref.shape[0]
+def gather_kernel(count, streams, *refs):
+    shards = refs[:streams]
+    fulls = refs[streams : 2 * streams]
+    own_sem, send_sem, recv_sem, pair_send, pair_recv = refs[2 * streams :]
+    rows = shards[0].shape[0]
     half = rows // 2
     core, place = ring_place(count)
     right, left, partner = neighbours(core, place, count)
     targets = (right, left)
-
-    def piece(way, step):
+    lanes = [(way, stream) for stream in range(streams) for way in range(2)]
+
+    def piece(way, step, stream):
         shift = count - step if way == 0 else step
         owner = chip_at((place + shift) % count, count) * 2 + core
-        return full_ref.at[pl.ds(pl.multiple_of(owner * rows + way * half, half), half)]
-
-    def hop(way, step):
-        ref = piece(way, step)
+        start = pl.multiple_of(owner * rows + way * half, half)
+        return fulls[stream].at[pl.ds(start, half)]
+
+    def hop(way, step, stream):
+        ref = piece(way, step, stream)
         return pltpu.make_async_remote_copy(
             src_ref=ref,
             dst_ref=ref,
-            send_sem=send_sem.at[way, step],
-            recv_sem=recv_sem.at[way, step],
+            send_sem=send_sem.at[stream, way, step],
+            recv_sem=recv_sem.at[stream, way, step],
             device_id={"dp": targets[way]},
             device_id_type=MESH,
         )
 
-    def share(way, step):
-        ref = piece(way, step)
+    def share(way, step, stream):
+        ref = piece(way, step, stream)
         return pltpu.make_async_remote_copy(
             src_ref=ref,
             dst_ref=ref,
-            send_sem=pair_send.at[way, step],
-            recv_sem=pair_recv.at[way, step],
+            send_sem=pair_send.at[stream, way, step],
+            recv_sem=pair_recv.at[stream, way, step],
             device_id={"dp": partner},
             device_id_type=MESH,
         )
 
     me = lax.axis_index("dp")
-    own = pltpu.make_async_copy(
-        shard_ref, full_ref.at[pl.ds(pl.multiple_of(me * rows, rows), rows)], own_sem
-    )
-    own.start()
+    owns = [
+        pltpu.make_async_copy(
+            shards[stream],
+            fulls[stream].at[pl.ds(pl.multiple_of(me * rows, rows), rows)],
+            own_sem.at[stream],
+        )
+        for stream in range(streams)
+    ]
+    for own in owns:
+        own.start()
     greet((right, left, partner))
-    own.wait()
-    for way in range(2):
-        hop(way, 0).start()
-        share(way, 0).start()
+    for own in owns:
+        own.wait()
+    for way, stream in lanes:
+        hop(way, 0, stream).start()
+        share(way, 0, stream).start()
 
     def step_body(step, carry):
-        for way in range(2):
-            hop(way, step - 1).wait_recv()
-            hop(way, step).start()
-            share(way, step).start()
+        for way, stream in lanes:
+            hop(way, step - 1, stream).wait_recv()
+            hop(way, step, stream).start()
+            share(way, step, stream).start()
         return carry
 
     lax.fori_loop(1, count - 1, step_body, 0)
-    for way in range(2):
-        hop(way, count - 2).wait_recv()
-        share(way, count - 1).start()
+    for way, stream in lanes:
+        hop(way, count - 2, stream).wait_recv()
+        share(way, count - 1, stream).start()
 
     def drain_hops(step, carry):
-        for way in range(2):
-            hop(way, step).wait_send()
+        for way, stream in lanes:
+            hop(way, step, stream).wait_send()
         return carry
 
     def drain_shares(step, carry):
-        for way in range(2):
-            share(way, step).wait_send()
-            share(way, step).wait_recv()
+        for way, stream in lanes:
+            share(way, step, stream).wait_send()
+            share(way, step, stream).wait_recv()
         return carry
 
     lax.fori_loop(0, count - 1, drain_hops, 0)
     lax.fori_loop(0, count, drain_shares, 0)
 
 
-def ring_gather(shard, devices):
+def ring_gather(shards, devices):
     count = devices // 2
-    rows, columns = shard.shape
+    streams = len(shards)
     return pl.pallas_call(
-        functools.partial(gather_kernel, count),
-        out_shape=jax.ShapeDtypeStruct((devices * rows, columns), shard.dtype),
-        in_specs=[pl.BlockSpec(memory_space=pltpu.VMEM)],
-        out_specs=pl.BlockSpec(memory_space=pltpu.HBM),
-        scratch_shapes=[
-            pltpu.SemaphoreType.DMA,
-            pltpu.SemaphoreType.DMA((2, count - 1)),
-            pltpu.SemaphoreType.DMA((2, count - 1)),
-            pltpu.SemaphoreType.DMA((2, count)),
-            pltpu.SemaphoreType.DMA((2, count)),
+        functools.partial(gather_kernel, count, streams),
+        out_shape=[
+            jax.ShapeDtypeStruct((devices * shard.shape[0], shard.shape[1]), shard.dtype)
+            for shard in shards
         ],
+        in_specs=[pl.BlockSpec(memory_space=pltpu.VMEM)] * streams,
+        out_specs=[pl.BlockSpec(memory_space=pl.ANY)] * streams,
+        scratch_shapes=[pltpu.SemaphoreType.DMA((streams,))]
+        + [pltpu.SemaphoreType.DMA((streams, 2, count - 1))] * 2
+        + [pltpu.SemaphoreType.DMA((streams, 2, count))] * 2,
+        cost_estimate=pl.CostEstimate(
+            flops=0, bytes_accessed=128 * 1024 * 1024, transcendentals=0
+        ),
         compiler_params=pltpu.CompilerParams(
-            collective_id=0, has_side_effects=True, vmem_limit_bytes=8 * 1024 * 1024
+            collective_id=0, has_side_effects=True, vmem_limit_bytes=VMEM_LIMIT
         ),
         name="ring_gather",
-    )(shard)
+    )(*shards)
 
 
 def scatter_kernel(count, streams, *refs):
@@ -352,7 +364,7 @@
         + [pltpu.SemaphoreType.DMA((streams, 2, count - 1))] * 2
         + [pltpu.SemaphoreType.DMA((streams, 2, count))] * 2,
         compiler_params=pltpu.CompilerParams(
-            collective_id=1, has_side_effects=True, vmem_limit_bytes=VMEM_LIMIT
+            collective_id=1, has_side_effects=True, vmem_limit_bytes=40 * 1024 * 1024
         ),
         name="ring_scatter",
     )(*grads)
@@ -704,8 +716,7 @@
         axis=1,
     )
     wide = second_pack.shape[1] // 3
-    first_full = ring_gather(first_pack, devices)
-    second_full = lax.all_gather(second_pack, "dp", axis=0, tiled=True)
+    first_full, second_full = ring_gather([first_pack, second_pack], devices)
     full_qkv = first_full[:, : 3 * local_width]
     full_out = first_full[:, 3 * local_width : 4 * local_width]
     gains = first_full[:, 4 * local_width : 4 * local_width + 4].astype(jnp.float32)
@@ -715,9 +726,10 @@
     full_down = second_full[:, 2 * wide :]
 
     inputs32 = layer_in.astype(jnp.float32)
-    normed_one, unit_one, inv_one = norm_forward(inputs32, gain_attn)
-    normed_full = rows_of_all(normed_one.astype(jnp.bfloat16))
+    all_inputs32 = rows_of_all(layer_in).astype(jnp.float32)
     cot_full = rows_of_all(cot_local)
+    normed_full = norm_forward(all_inputs32, gain_attn)[0].astype(jnp.bfloat16)
+    unit_one, inv_one = norm_forward(inputs32, gain_attn)[1:]
     if paired:
         seg_full = rows_of_all(
             jnp.broadcast_to(seg_local.astype(jnp.float32)[:, None], (own_rows, LANES))
@@ -745,7 +757,6 @@
     layer_out = (residual + sum_to_owner(dot(middle_b, full_down, 1, 1))).astype(jnp.bfloat16)
 
     down_grad = dot(cot_full, middle_b, 0, 0).astype(jnp.bfloat16)
-    down_share = lax.psum_scatter(down_grad, "dp", scatter_dimension=0, tiled=True)
     dmiddle = dot(cot_full, full_down, 1, 0)
     dexpanded_b = jnp.concatenate(
         [dmiddle * linear_in * gelu_slope(gate_in), dmiddle * activated], axis=1
@@ -765,8 +776,8 @@
     gain_sums = sum_over_seq(jnp.stack([attn_gain_part, mlp_gain_part]))
     gain_grad = padded_to_lanes(gain_sums.T).astype(jnp.bfloat16)
 
-    in_share, qkv_share, out_share, gain_share = ring_scatter(
-        [in_grad, qkv_grad, out_grad, gain_grad], devices
+    in_share, qkv_share, down_share, out_share, gain_share = ring_scatter(
+        [in_grad, qkv_grad, down_grad, out_grad, gain_grad], devices
     )
     return (
         layer_out[None],
@@ -774,7 +785,7 @@
         qkv_share.reshape(shard_rows, 3, local_width),
         out_share.T,
         jnp.stack([in_share[:, :local_hidden], in_share[:, wide : wide + local_hidden]], axis=1),
-        down_share.astype(jnp.float32)[:, :local_hidden].T,
+        down_share[:, :local_hidden].T,
         gain_share[:, 0],
         gain_share[:, 1],
     )

time: 240 us -> 231 us (0.963)
  Pallas kernels: 133 us -> 147 us
  between operations: 14.6 us -> 1.06 us
  matrix products: 25.7 us -> 20.7 us
  local copies, waits for them, and re-layouts: 13.3 us -> 10.9 us
    pallas_call x1, Pallas kernels: 56.4 us -> 69.3 us  [ring_gather(): pl.pallas_call(functools.partial(gather_kernel, count, streams), out_shap...]
    ppermute x5, waiting for transfers between devices: 15.5 us -> 9.63 us  [rows_of_all(): return jnp.concatenate([values, lax.ppermute(values, 'seq', swap)], axis=0)]
    dot_general x12, matrix products: 25.7 us -> 20.7 us  [dot(): lax.dot_general(left, right, (((left_dim,), (right_dim,)), ((), ())), pre...]
    ppermute x4, waiting for transfers between devices: 13.1 us -> 17.1 us  [sum_to_owner(): other = lax.ppermute(partial[own_rows:].astype(jnp.bfloat16), 'seq', swap)]
    unnamed x60 -> x24, local copies, waits for them, and re-layouts: 4.94 us -> 5.22 us
  transfers between devices with their start and end apart: 12 -> 10, of which waited for: 8 -> 7; matrix products, arithmetic and copies ran while one was open for 15% -> 10% of each run, Pallas kernels for 56% -> 30%
where the time goes in v2:
time: 231 us; the launch traced here: 230 us
  Pallas kernels  147 us (64%)
  waiting for transfers between devices  28.5 us (12%)
  matrix products  20.7 us (9%)
  starting transfers between devices  12.4 us (5%)
  local copies, waits for them, and re-layouts  10.9 us (5%)
  other arithmetic  9.59 us (4%)
    pallas_call x1, Pallas kernels, ring_scatter(): pl.pallas_call(functools.partial(scatter_kernel, count, streams), out_sha...  72.3 us
    pallas_call x1, Pallas kernels, ring_gather(): pl.pallas_call(functools.partial(gather_kernel, count, streams), out_shap...  69.3 us
    dot_general x12, matrix products, dot(): lax.dot_general(left, right, (((left_dim,), (right_dim,)), ((), ())), pre...  20.7 us
    ppermute x4, waiting for transfers between devices, sum_to_owner(): other = lax.ppermute(partial[own_rows:].astype(jnp.bfloat16), 'seq', swap)  17.1 us
    ppermute x5, waiting for transfers between devices, rows_of_all(): return jnp.concatenate([values, lax.ppermute(values, 'seq', swap)], axis=0)  9.63 us
    ppermute x5, starting transfers between devices, rows_of_all(): return jnp.concatenate([values, lax.ppermute(values, 'seq', swap)], axis=0)  6.7 us
    pallas_call x2, Pallas kernels, local_call(): pl.pallas_call(kernel, out_shape=out_shape, in_specs=[vmem] * len(operand...  5.7 us
    unnamed x24, local copies, waits for them, and re-layouts  5.22 us
  transfers between devices with their start and end apart: 10, of which 7 were waited for; matrix products, arithmetic and copies ran while one was open for 10% of the time, Pallas kernels for 30%

profile of v2, /device:TPU:0, one launch (start us, length us, event | category | flops | bytes accessed | tf_op | source)
XLA Modules:
  0.0 230.4 jit_solution(4326996105861780978)
XLA Ops:
  1.4 3.0 %collective-permute-start.1 = (f32[128,128]{1,0:T(8,128)S(1)}, f32[128,128]{1,0:T(8,128)S(1)}, u32[]{:S(2)}, u32[]{:S(2)}) collective-permute-start(f32[128,128]{1,0:T(8,128)S(1)} %broadcast_in_dim.24), channel_id=1, source_target_pairs={{0,1},{1,0},{2,3},{3,2},{4,5},{5,4},{6,7},{7,6},{8,9},{9,8},{10,11... | collective-permute-start | bytes 196616 | tf_op jit(solution)/shard_map/ppermute | solution.py:685
  6.4 1.7 fusion.67
  9.7 69.3 %ring_gather.1 = (bf16[1024,2176]{1,0:T(8,128)(2,1)}, bf16[1024,4224]{1,0:T(8,128)(2,1)}) custom-call(bf16[64,2176]{1,0:T(8,128)(2,1)} %fusion.49.refs_0_, bf16[64,4224]{1,0:T(8,128)(2,1)} %fusion.37.refs_1_), custom_call_target="tpu_custom_call" | custom-call | bytes 134217728 | tf_op jit(solution)/shard_map/ring_gather/pallas_call | solution.py:238
  79.0 1.0 slice_convert_fusion.4
  82.5 3.1 %fusion.6.proj = f32[256,1536]{1,0:T(8,128)S(1)} fusion(bf16[1024,2176]{1,0:T(8,128)(2,1)} %get-tuple-element.17, f32[1024]{0:T(1024)S(1)} %get-tuple-element.65, f32[256]{0:T(256)S(1)} %add_rsqrt_fusion, f32[256]{0:T(256)S(1)} %broadcast_multiply_fusion, bf16[128,1024]{1,0:T(8,128)(2,1)S(1)} %collective-permute-done, bf16[128,1024]{1,0:T(8,128)(2,1)S(1)} %bitcast.66), kind=kOutput, calls=%fused_computation.9 | convolution fusion | flops 807403520 | bytes 5249024 | tf_op jit(solution)/shard_map/dot_general | solution.py:636
  85.7 2.5 %attend.1 = (bf16[256,1536]{1,0:T(8,128)(2,1)S(1)}, bf16[256,512]{1,0:T(8,128)(2,1)S(1)}) custom-call(f32[256,1536]{1,0:T(8,128)S(1)} %fusion.6.proj, f32[256,128]{1,0:T(8,128)S(1)} %pad_maximum_fusion.15.cos_ref, f32[256,128]{1,0:T(8,128)S(1)} %pad_maximum_fusion.16.sin_ref, s32[256,1]{1,0:T(8,128)S(1)} %copy.54.pos_col, s32[1,256]{1,0:T(1,128)S(1)} %bitcast.59, ...), custom_call_target="tpu_custom_call" | custom-call | flops 268435456 | bytes 4194304 | tf_op jit(solution)/shard_map/attend/pallas_call | solution.py:498
  88.7 1.6 collective-permute-start.2
  90.4 6.9 %collective-permute-done.2 = bf16[128,1024]{1,0:T(8,128)(2,1)S(1)} collective-permute-done((bf16[128,1024]{1,0:T(8,128)(2,1)S(1)}, bf16[128,1024]{1,0:T(8,128)(2,1)S(1)}, u32[]{:S(2)}, u32[]{:S(2)}) %collective-permute-start.2) | collective-permute-done | bytes 262176 | tf_op jit(solution)/shard_map/ppermute | solution.py:690
  98.0 1.6 collective-permute-start.3
  100.1 7.1 %collective-permute-done.3 = bf16[128,1024]{1,0:T(8,128)(2,1)S(1)} collective-permute-done((bf16[128,1024]{1,0:T(8,128)(2,1)S(1)}, bf16[128,1024]{1,0:T(8,128)(2,1)S(1)}, u32[]{:S(2)}, u32[]{:S(2)}) %collective-permute-start.3) | collective-permute-done | bytes 262176 | tf_op jit(solution)/shard_map/ppermute | solution.py:685
  107.2 1.7 fusion.2
  108.9 2.5 %collective-permute-done.5 = bf16[128,1024]{1,0:T(8,128)(2,1)S(1)} collective-permute-done((bf16[128,1024]{1,0:T(8,128)(2,1)S(1)}, bf16[128,1024]{1,0:T(8,128)(2,1)S(1)}, u32[]{:S(2)}, u32[]{:S(2)}) %collective-permute-start.5) | collective-permute-done | bytes 262176 | tf_op jit(solution)/shard_map/ppermute | solution.py:685
  111.4 1.5 fusion.17
  112.8 1.7 fusion
  114.6 1.6 collective-permute-start.6
  116.1 1.0 fusion.10
  117.8 6.0 %collective-permute-done.6 = bf16[128,1024]{1,0:T(8,128)(2,1)S(1)} collective-permute-done((bf16[128,1024]{1,0:T(8,128)(2,1)S(1)}, bf16[128,1024]{1,0:T(8,128)(2,1)S(1)}, u32[]{:S(2)}, u32[]{:S(2)}) %collective-permute-start.6) | collective-permute-done | bytes 262176 | tf_op jit(solution)/shard_map/ppermute | solution.py:690
  124.1 3.0 %collective-permute-done.4 = bf16[128,1024]{1,0:T(8,128)(2,1)S(1)} collective-permute-done((bf16[128,1024]{1,0:T(8,128)(2,1)S(1)}, bf16[128,1024]{1,0:T(8,128)(2,1)S(1)}, u32[]{:S(2)}, u32[]{:S(2)}) %collective-permute-start.4) | collective-permute-done | bytes 262176 | tf_op jit(solution)/shard_map/ppermute | solution.py:690
  128.0 1.5 collective-permute-start.7
  129.5 1.2 convolution_convert_fusion.1.refs_2_
  130.8 4.2 %convolution_convert_fusion.refs_0_ = bf16[1024,2816]{1,0:T(8,128)(2,1)} fusion(bf16[256,1408]{1,0:T(8,128)(2,1)S(1)} %get-tuple-element.73, bf16[256,1408]{1,0:T(8,128)(2,1)S(1)} %get-tuple-element.72, bf16[128,1024]{1,0:T(8,128)(2,1)S(1)} %collective-permute-done.3, bf16[128,1024]{1,0:T(8,128)(2,1)S(1)} %multiply_convert_fusion.2), kind=kOutput, calls=%fused_computation | convolution fusion | flops 1483210752 | bytes 7733248 | tf_op jit(solution)/shard_map/dot_general | solution.py:636
  135.4 3.2 %attend_back.1 = bf16[256,1536]{1,0:T(8,128)(2,1)S(1)} custom-call(bf16[256,1536]{1,0:T(8,128)(2,1)S(1)} %get-tuple-element.20.qkv, bf16[256,512]{1,0:T(8,128)(2,1)S(1)} %get-tuple-element.18.mixed_ref, bf16[256,512]{1,0:T(8,128)(2,1)S(1)} %convolution_convert_fusion.4.dmixed_ref, f32[256,128]{1,0:T(8,128)S(1)} %pad_maximum_fusion.15.cos_ref, ...), custom_call_target="tpu_custom_call" | custom-call | flops 671088640 | bytes 4194304 | tf_op jit(solution)/shard_map/attend_back/pallas_call | solution.py:498
  138.7 1.0 fusion.4
  140.7 2.9 %convolution_convert_fusion.2.refs_1_ = bf16[1024,1536]{1,0:T(8,128)(2,1)} fusion(bf16[256,1536]{1,0:T(8,128)(2,1)S(1)} %attend_back.1, f32[1024]{0:T(1024)S(1)} %get-tuple-element.65, f32[256]{0:T(256)S(1)} %add_rsqrt_fusion, f32[256]{0:T(256)S(1)} %broadcast_multiply_fusion, bf16[128,1024]{1,0:T(8,128)(2,1)S(1)} %copy-done.5, ...), kind=kOutput, calls=%fused_computation.6 | convolution fusion | flops 808976384 | bytes 4462592 | tf_op jit(solution)/shard_map/dot_general | solution.py:636
  143.6 1.5 convolution_convert_fusion.3.refs_3_
  145.1 1.2 collective-permute-done.8
  147.6 1.0 fusion.51
  148.6 1.7 collective-permute-done.9
  150.6 1.9 copy-done
  152.5 1.2 copy-done.1
  153.7 72.3 %ring_scatter.1 = (f32[64,2816]{1,0:T(8,128)S(1)}, f32[64,1536]{1,0:T(8,128)S(1)}, f32[64,1408]{1,0:T(8,128)S(1)}, f32[64,512]{1,0:T(8,128)S(1)}, f32[64,128]{1,0:T(8,128)S(1)}) custom-call(bf16[1024,2816]{1,0:T(8,128)(2,1)} %convolution_convert_fusion.refs_0_, bf16[1024,1536]{1,0:T(8,128)(2,1)S(1)} %copy-done, ...), custom_call_target="tpu_custom_call" | custom-call | tf_op jit(solution)/shard_map/ring_scatter/pallas_call | solution.py:357
  228.3 1.4 copy.58
  (83 shorter events, 16.3 us)
Async XLA Ops:
  0.6 7.5 %copy-start.7 = (bf16[512,64]{0,1:T(8,128)(2,1)S(1)}, bf16[512,64]{0,1:T(8,128)(2,1)}, u32[]{:S(2)}) copy-start(bf16[512,64]{0,1:T(8,128)(2,1)} %param.13) | copy-start | bytes 196612
  0.6 8.3 %copy-start.6 = (bf16[1312,64]{0,1:T(8,128)(2,1)S(1)}, bf16[1312,64]{0,1:T(8,128)(2,1)}, u32[]{:S(2)}) copy-start(bf16[1312,64]{0,1:T(8,128)(2,1)} %param.15) | copy-start | bytes 503812
  1.4 80.4 %collective-permute-start.1 = (f32[128,128]{1,0:T(8,128)S(1)}, f32[128,128]{1,0:T(8,128)S(1)}, u32[]{:S(2)}, u32[]{:S(2)}) collective-permute-start(f32[128,128]{1,0:T(8,128)S(1)} %broadcast_in_dim.24), channel_id=1, source_target_pairs={{0,1},{1,0},{2,3},{3,2},{4,5},{5,4},{6,7},{7,6},{8,9},{9,8},{10,11... | collective-permute-start | bytes 196616 | tf_op jit(solution)/shard_map/ppermute | solution.py:685
  4.5 77.5 %collective-permute-start = (bf16[128,1024]{1,0:T(8,128)(2,1)}, bf16[128,1024]{1,0:T(8,128)(2,1)S(1)}, u32[]{:S(2)}, u32[]{:S(2)}) collective-permute-start(bf16[128,1024]{1,0:T(8,128)(2,1)} %bitcast.63), channel_id=1, source_target_pairs={{0,1},{1,0},{2,3},{3,2},{4,5},{5,4},{6,7},{7,6},{8,9},{9,8},{10,11... | collective-permute-start | bytes 786440 | tf_op jit(solution)/shard_map/ppermute | solution.py:685
  9.7 72.3 %copy-start.2 = (bf16[1,128,1024]{2,1,0:T(8,128)(2,1)S(1)}, bf16[1,128,1024]{2,1,0:T(8,128)(2,1)}, u32[]{:S(2)}) copy-start(bf16[1,128,1024]{2,1,0:T(8,128)(2,1)} %param.9) | copy-start | bytes 786436
  82.0 3.6 %copy-start.4 = (bf16[128,1024]{1,0:T(8,128)(2,1)}, bf16[128,1024]{1,0:T(8,128)(2,1)S(1)}, u32[]{:S(2)}) copy-start(bf16[128,1024]{1,0:T(8,128)(2,1)S(1)} %collective-permute-done) | copy-start | bytes 786436
  82.2 5.9 %slice-start = ((s8[4456448]{0:T(1024)(128)(4,1)}), s8[4194304]{0:T(1024)(128)(4,1)S(1)}, s32[]{:S(2)}) async-start(s8[4456448]{0:T(1024)(128)(4,1)} %bitcast.74), calls=%async_computation | async-start | bytes 8388608
  82.5 5.7 %slice-start.1 = ((s8[4456448]{0:T(1024)(128)(4,1)}), s8[262144]{0:T(1024)(128)(4,1)S(1)}, s32[]{:S(2)}) async-start(s8[4456448]{0:T(1024)(128)(4,1)} %bitcast.74), calls=%async_computation.1 | async-start | bytes 524288
  82.5 24.7 %copy-start.8 = (bf16[1024,4224]{1,0:T(8,128)(2,1)S(1)}, bf16[1024,4224]{1,0:T(8,128)(2,1)}, u32[]{:S(2)}) copy-start(bf16[1024,4224]{1,0:T(8,128)(2,1)} %get-tuple-element.19) | copy-start | bytes 25952260
  88.2 11.4 %copy-start.3 = (bf16[1,128,1024]{2,1,0:T(8,128)(2,1)S(1)}, bf16[1,128,1024]{2,1,0:T(8,128)(2,1)}, u32[]{:S(2)}) copy-start(bf16[1,128,1024]{2,1,0:T(8,128)(2,1)} %param.11) | copy-start | bytes 786436
  88.7 8.7 %collective-permute-start.2 = (bf16[128,1024]{1,0:T(8,128)(2,1)S(1)}, bf16[128,1024]{1,0:T(8,128)(2,1)S(1)}, u32[]{:S(2)}, u32[]{:S(2)}) collective-permute-start(bf16[128,1024]{1,0:T(8,128)(2,1)S(1)} %slice.206), channel_id=1, source_target_pairs={{0,1},{1,0},{2,3},{3,2},{4,5},{5,4},{6,7},{7,6},{8,9},{9,8},{10,11... | collective-permute-start | bytes 786440 | tf_op jit(solution)/shard_map/ppermute | solution.py:690
  98.0 9.2 %collective-permute-start.3 = (bf16[128,1024]{1,0:T(8,128)(2,1)S(1)}, bf16[128,1024]{1,0:T(8,128)(2,1)S(1)}, u32[]{:S(2)}, u32[]{:S(2)}) collective-permute-start(bf16[128,1024]{1,0:T(8,128)(2,1)S(1)} %multiply_convert_fusion.2), channel_id=1, source_target_pairs={{0,1},{1,0},{2,3},{3,2},{4,5},{5,4},{6,7},{7,6},{8,9},{9,8},{10,11... | collective-permute-start | bytes 786440 | tf_op jit(solution)/shard_map/ppermute | solution.py:685
  99.5 11.8 %collective-permute-start.5 = (bf16[128,1024]{1,0:T(8,128)(2,1)S(1)}, bf16[128,1024]{1,0:T(8,128)(2,1)S(1)}, u32[]{:S(2)}, u32[]{:S(2)}) collective-permute-start(bf16[128,1024]{1,0:T(8,128)(2,1)S(1)} %bitcast.68), channel_id=1, source_target_pairs={{0,1},{1,0},{2,3},{3,2},{4,5},{5,4},{6,7},{7,6},{8,9},{9,8},{10,11... | collective-permute-start | bytes 786440 | tf_op jit(solution)/shard_map/ppermute | solution.py:685
  114.6 9.2 %collective-permute-start.6 = (bf16[128,1024]{1,0:T(8,128)(2,1)S(1)}, bf16[128,1024]{1,0:T(8,128)(2,1)S(1)}, u32[]{:S(2)}, u32[]{:S(2)}) collective-permute-start(bf16[128,1024]{1,0:T(8,128)(2,1)S(1)} %slice.204), channel_id=1, source_target_pairs={{0,1},{1,0},{2,3},{3,2},{4,5},{5,4},{6,7},{7,6},{8,9},{9,8},{10,11... | collective-permute-start | bytes 786440 | tf_op jit(solution)/shard_map/ppermute | solution.py:690
  117.2 9.9 %collective-permute-start.4 = (bf16[128,1024]{1,0:T(8,128)(2,1)S(1)}, bf16[128,1024]{1,0:T(8,128)(2,1)S(1)}, u32[]{:S(2)}, u32[]{:S(2)}) collective-permute-start(bf16[128,1024]{1,0:T(8,128)(2,1)S(1)} %slice.205), channel_id=1, source_target_pairs={{0,1},{1,0},{2,3},{3,2},{4,5},{5,4},{6,7},{7,6},{8,9},{9,8},{10,11... | collective-permute-start | bytes 786440 | tf_op jit(solution)/shard_map/ppermute | solution.py:690
  128.0 7.0 %collective-permute-start.7 = (bf16[128,1024]{1,0:T(8,128)(2,1)S(1)}, bf16[128,1024]{1,0:T(8,128)(2,1)S(1)}, u32[]{:S(2)}, u32[]{:S(2)}) collective-permute-start(bf16[128,1024]{1,0:T(8,128)(2,1)S(1)} %get-tuple-element.68), channel_id=1, source_target_pairs={{0,1},{1,0},{2,3},{3,2},{4,5},{5,4},{6,7},{7,6},{8,9},{9,8},{10,11... | collective-permute-start | bytes 786440 | tf_op jit(solution)/shard_map/ppermute | solution.py:685
  138.7 2.0 copy-start.5
  139.7 6.5 %collective-permute-start.8 = (bf16[128,1024]{1,0:T(8,128)(2,1)S(1)}, bf16[128,1024]{1,0:T(8,128)(2,1)S(1)}, u32[]{:S(2)}, u32[]{:S(2)}) collective-permute-start(bf16[128,1024]{1,0:T(8,128)(2,1)S(1)} %slice.203), channel_id=1, source_target_pairs={{0,1},{1,0},{2,3},{3,2},{4,5},{5,4},{6,7},{7,6},{8,9},{9,8},{10,11... | collective-permute-start | bytes 786440 | tf_op jit(solution)/shard_map/ppermute | solution.py:690
  146.6 3.7 %collective-permute-start.9 = (f32[2,1024]{1,0:T(2,128)S(1)}, f32[2,1024]{1,0:T(2,128)S(1)}, u32[]{:S(2)}, u32[]{:S(2)}) collective-permute-start(f32[2,1024]{1,0:T(2,128)S(1)} %pad_maximum_fusion.17), channel_id=1, source_target_pairs={{0,1},{1,0},{2,3},{3,2},{4,5},{5,4},{6,7},{7,6},{8,9},{9,8},{10,11... | collective-permute-start | bytes 24584 | tf_op jit(solution)/shard_map/ppermute | solution.py:698
  150.6 1.9 copy-start
  152.5 1.2 copy-start.1

commit v3 on v2

--- a/solution.py
+++ b/solution.py
@@ -699,35 +699,35 @@
         return lax.psum(part, "seq")
 
     first_pack = jnp.concatenate(
-        [qkv_weight.reshape(shard_rows, 3 * local_width), out_weight.T]
-        + [
-            padded_to_lanes(
-                jnp.concatenate(high_and_low(attn_gain) + high_and_low(mlp_gain), axis=1)
-            )
-        ],
+        [qkv_weight.reshape(shard_rows, 3 * local_width), out_weight.T], axis=1
+    )
+    wide = (local_hidden + 4 + LANES - 1) // LANES * LANES
+    spare = jnp.zeros((shard_rows, wide - local_hidden), jnp.bfloat16)
+    second_pack = jnp.concatenate(
+        [in_weight[:, 0, :], spare, in_weight[:, 1, :], spare, down_weight.T]
+        + high_and_low(attn_gain)
+        + high_and_low(mlp_gain)
+        + [spare[:, 4:]],
         axis=1,
     )
-    second_pack = jnp.concatenate(
-        [
-            padded_to_lanes(in_weight[:, 0, :]),
-            padded_to_lanes(in_weight[:, 1, :]),
-            padded_to_lanes(down_weight.T),
-        ],
-        axis=1,
-    )
-    wide = second_pack.shape[1] // 3
     first_full, second_full = ring_gather([first_pack, second_pack], devices)
     full_qkv = first_full[:, : 3 * local_width]
     full_out = first_full[:, 3 * local_width : 4 * local_width]
-    gains = first_full[:, 4 * local_width : 4 * local_width + 4].astype(jnp.float32)
+    gains_at = 2 * wide + local_hidden
+    gains = second_full[:, gains_at : gains_at + 4].astype(jnp.float32)
     gain_attn = gains[:, 0] + gains[:, 1]
     gain_mlp = gains[:, 2] + gains[:, 3]
     full_in = second_full[:, : 2 * wide]
     full_down = second_full[:, 2 * wide :]
 
     inputs32 = layer_in.astype(jnp.float32)
-    all_inputs32 = rows_of_all(layer_in).astype(jnp.float32)
-    cot_full = rows_of_all(cot_local)
+    if paired:
+        arrived = lax.ppermute(jnp.concatenate([layer_in, cot_local], axis=0), "seq", swap)
+        all_inputs32 = jnp.concatenate([layer_in, arrived[:own_rows]], axis=0).astype(jnp.float32)
+        cot_full = jnp.concatenate([cot_local, arrived[own_rows:]], axis=0)
+    else:
+        all_inputs32 = rows_of_all(layer_in).astype(jnp.float32)
+        cot_full = rows_of_all(cot_local)
     normed_full = norm_forward(all_inputs32, gain_attn)[0].astype(jnp.bfloat16)
     unit_one, inv_one = norm_forward(inputs32, gain_attn)[1:]
     if paired:
@@ -754,7 +754,7 @@
     linear_in = expanded[:, wide:]
     activated = gelu_value(gate_in)
     middle_b = (activated * linear_in).astype(jnp.bfloat16)
-    layer_out = (residual + sum_to_owner(dot(middle_b, full_down, 1, 1))).astype(jnp.bfloat16)
+    down_part = dot(middle_b, full_down, 1, 1)
 
     down_grad = dot(cot_full, middle_b, 0, 0).astype(jnp.bfloat16)
     dmiddle = dot(cot_full, full_down, 1, 0)
@@ -766,9 +766,12 @@
     dres_norm, mlp_gain_part = norm_backward(dnormed_two, gain_mlp, unit_two, inv_two)
     dresidual = cot_local.astype(jnp.float32) + dres_norm
     dres_full = rows_of_all(dresidual.astype(jnp.bfloat16))
+    down_part, dres_full = lax.optimization_barrier((down_part, dres_full))
+    layer_out = (residual + sum_to_owner(down_part)).astype(jnp.bfloat16)
     dmixed = dot(dres_full, full_out, 1, 0).astype(jnp.bfloat16)
     out_grad = dot(dres_full, mixed, 0, 0).astype(jnp.bfloat16)
     dqkv_b = attention.backward(dmixed)
+    layer_out, dqkv_b = lax.optimization_barrier((layer_out, dqkv_b))
     dnormed_one = sum_to_owner(dot(dqkv_b, full_qkv, 1, 1))
     qkv_grad = dot(normed_full, dqkv_b, 0, 0).astype(jnp.bfloat16)
     dinput_norm, attn_gain_part = norm_backward(dnormed_one, gain_attn, unit_one, inv_one)

time: 231 us -> 225 us (0.974)
  waiting for transfers between devices: 28.5 us -> 22.5 us
    ppermute x5 -> x3, waiting for transfers between devices: 9.63 us -> 6.2 us  [rows_of_all(): return jnp.concatenate([values, lax.ppermute(values, 'seq', swap)], axis=0)]
    ppermute x4, waiting for transfers between devices: 17.1 us -> 14.6 us  [sum_to_owner(): other = lax.ppermute(partial[own_rows:].astype(jnp.bfloat16), 'seq', swap)]
    ppermute x5 -> x3, starting transfers between devices: 6.7 us -> 6.2 us  [rows_of_all(): return jnp.concatenate([values, lax.ppermute(values, 'seq', swap)], axis=0)]
    unnamed x24 -> x22, local copies, waits for them, and re-layouts: 5.22 us -> 5.58 us
  transfers between devices with their start and end apart: 10 -> 9, of which waited for: 7 -> 6; matrix products, arithmetic and copies ran while one was open for 10% -> 10% of each run, Pallas kernels for 30% -> 32%
where the time goes in v3:
time: 225 us; the launch traced here: 224 us
  Pallas kernels  146 us (65%)
  waiting for transfers between devices  22.5 us (10%)
  matrix products  18.7 us (8%)
  local copies, waits for them, and re-layouts  12.6 us (6%)
  starting transfers between devices  12.4 us (6%)
  other arithmetic  10.9 us (5%)
    pallas_call x1, Pallas kernels, ring_scatter(): pl.pallas_call(functools.partial(scatter_kernel, count, streams), out_sha...  72.3 us
    pallas_call x1, Pallas kernels, ring_gather(): pl.pallas_call(functools.partial(gather_kernel, count, streams), out_shap...  68 us
    dot_general x12, matrix products, dot(): lax.dot_general(left, right, (((left_dim,), (right_dim,)), ((), ())), pre...  18.7 us
    ppermute x4, waiting for transfers between devices, sum_to_owner(): other = lax.ppermute(partial[own_rows:].astype(jnp.bfloat16), 'seq', swap)  14.6 us
    ppermute x3, waiting for transfers between devices, rows_of_all(): return jnp.concatenate([values, lax.ppermute(values, 'seq', swap)], axis=0)  6.2 us
    ppermute x3, starting transfers between devices, rows_of_all(): return jnp.concatenate([values, lax.ppermute(values, 'seq', swap)], axis=0)  6.2 us
    pallas_call x2, Pallas kernels, local_call(): pl.pallas_call(kernel, out_shape=out_shape, in_specs=[vmem] * len(operand...  5.75 us
    unnamed x22, local copies, waits for them, and re-layouts  5.58 us
  transfers between devices with their start and end apart: 9, of which 6 were waited for; matrix products, arithmetic and copies ran while one was open for 10% of the time, Pallas kernels for 32%

profile of v3, /device:TPU:0, one launch (start us, length us, event | category | flops | bytes accessed | tf_op | source)
XLA Modules:
  0.0 224.4 jit_solution(3050793942799126017)
XLA Ops:
  1.4 3.0 %collective-permute-start.1 = (f32[128,128]{1,0:T(8,128)S(1)}, f32[128,128]{1,0:T(8,128)S(1)}, u32[]{:S(2)}, u32[]{:S(2)}) collective-permute-start(f32[128,128]{1,0:T(8,128)S(1)} %broadcast_in_dim.27), channel_id=1, source_target_pairs={{0,1},{1,0},{2,3},{3,2},{4,5},{5,4},{6,7},{7,6},{8,9},{9,8},{10,11... | collective-permute-start | bytes 196616 | tf_op jit(solution)/shard_map/ppermute | solution.py:685
  4.5 1.1 pad_maximum_fusion.4
  8.5 1.7 fusion.55
  12.0 68.0 %ring_gather.1 = (bf16[1024,2048]{1,0:T(8,128)(2,1)}, bf16[1024,4224]{1,0:T(8,128)(2,1)}) custom-call(bf16[64,2048]{1,0:T(8,128)(2,1)} %pad_maximum_fusion.13.refs_0_, bf16[64,4224]{1,0:T(8,128)(2,1)} %concatenate.44.refs_1_), custom_call_target="tpu_custom_call" | custom-call | bytes 134217728 | tf_op jit(solution)/shard_map/ring_gather/pallas_call | solution.py:238
  80.1 1.1 slice_convert_fusion.4
  84.1 1.1 fusion.6.proj
  85.3 2.5 %attend.1 = (bf16[256,1536]{1,0:T(8,128)(2,1)S(1)}, bf16[256,512]{1,0:T(8,128)(2,1)S(1)}) custom-call(f32[256,1536]{1,0:T(8,128)S(1)} %fusion.6.proj, f32[256,128]{1,0:T(8,128)S(1)} %pad_maximum_fusion.15.cos_ref, f32[256,128]{1,0:T(8,128)S(1)} %pad_maximum_fusion.16.sin_ref, s32[256,1]{1,0:T(8,128)S(1)} %copy.60.pos_col, s32[1,256]{1,0:T(1,128)S(1)} %bitcast.60, ...), custom_call_target="tpu_custom_call" | custom-call | flops 268435456 | bytes 4194304 | tf_op jit(solution)/shard_map/attend/pallas_call | solution.py:498
  88.3 1.6 collective-permute-start.2
  90.0 6.9 %collective-permute-done.2 = bf16[128,1024]{1,0:T(8,128)(2,1)S(1)} collective-permute-done((bf16[128,1024]{1,0:T(8,128)(2,1)S(1)}, bf16[128,1024]{1,0:T(8,128)(2,1)S(1)}, u32[]{:S(2)}, u32[]{:S(2)}) %collective-permute-start.2) | collective-permute-done | bytes 262176 | tf_op jit(solution)/shard_map/ppermute | solution.py:690
  97.5 1.6 collective-permute-start.3
  99.1 6.2 %collective-permute-done.3 = bf16[128,1024]{1,0:T(8,128)(2,1)S(1)} collective-permute-done((bf16[128,1024]{1,0:T(8,128)(2,1)S(1)}, bf16[128,1024]{1,0:T(8,128)(2,1)S(1)}, u32[]{:S(2)}, u32[]{:S(2)}) %collective-permute-start.3) | collective-permute-done | bytes 262176 | tf_op jit(solution)/shard_map/ppermute | solution.py:685
  105.3 1.7 fusion.2
  107.0 1.4 fusion.17
  108.5 1.7 fusion
  110.2 1.6 collective-permute-start.4
  111.8 1.0 fusion.10
  112.8 4.3 %collective-permute-done.4 = bf16[128,1024]{1,0:T(8,128)(2,1)S(1)} collective-permute-done((bf16[128,1024]{1,0:T(8,128)(2,1)S(1)}, bf16[128,1024]{1,0:T(8,128)(2,1)S(1)}, u32[]{:S(2)}, u32[]{:S(2)}) %collective-permute-start.4) | collective-permute-done | bytes 262176 | tf_op jit(solution)/shard_map/ppermute | solution.py:690
  117.7 1.6 collective-permute-start.5
  119.3 1.2 convolution_convert_fusion.1.refs_2_
  120.6 4.2 %convolution_convert_fusion.refs_0_ = bf16[1024,2816]{1,0:T(8,128)(2,1)} fusion(bf16[256,1408]{1,0:T(8,128)(2,1)S(1)} %get-tuple-element.81, bf16[256,1408]{1,0:T(8,128)(2,1)S(1)} %get-tuple-element.80, bf16[128,1024]{1,0:T(8,128)(2,1)S(1)} %collective-permute-done.3, bf16[128,1024]{1,0:T(8,128)(2,1)S(1)} %multiply_convert_fusion.2), kind=kOutput, calls=%fused_computation | convolution fusion | flops 1483210752 | bytes 7733248 | tf_op jit(solution)/shard_map/dot_general | solution.py:636
  125.3 1.0 collective-permute-start.6
  126.3 3.3 %attend_back.1 = bf16[256,1536]{1,0:T(8,128)(2,1)S(1)} custom-call(bf16[256,1536]{1,0:T(8,128)(2,1)S(1)} %get-tuple-element.25.qkv, bf16[256,512]{1,0:T(8,128)(2,1)S(1)} %get-tuple-element.23.mixed_ref, bf16[256,512]{1,0:T(8,128)(2,1)S(1)} %convolution_convert_fusion.4.dmixed_ref, f32[256,128]{1,0:T(8,128)S(1)} %pad_maximum_fusion.15.cos_ref, ...), custom_call_target="tpu_custom_call" | custom-call | flops 671088640 | bytes 4194304 | tf_op jit(solution)/shard_map/attend_back/pallas_call | solution.py:498
  129.6 1.5 convolution_convert_fusion.3.refs_3_
  132.6 1.1 fusion.4
  134.7 2.9 %convolution_convert_fusion.2.refs_1_ = bf16[1024,1536]{1,0:T(8,128)(2,1)} fusion(bf16[256,1536]{1,0:T(8,128)(2,1)S(1)} %attend_back.1, f32[1024]{0:T(1024)S(1)} %get-tuple-element.73, f32[256]{0:T(256)S(1)} %add_rsqrt_fusion, f32[256]{0:T(256)S(1)} %broadcast_multiply_fusion, bf16[128,1024]{1,0:T(8,128)(2,1)S(1)} %get-tuple-element.86, ...), kind=kOutput, calls=%fused_computation.6 | convolution fusion | flops 808976384 | bytes 4462592 | tf_op jit(solution)/shard_map/dot_general | solution.py:636
  137.5 2.7 %collective-permute-done.7 = bf16[128,1024]{1,0:T(8,128)(2,1)S(1)} collective-permute-done((bf16[128,1024]{1,0:T(8,128)(2,1)S(1)}, bf16[128,1024]{1,0:T(8,128)(2,1)S(1)}, u32[]{:S(2)}, u32[]{:S(2)}) %collective-permute-start.7) | collective-permute-done | bytes 262176 | tf_op jit(solution)/shard_map/ppermute | solution.py:690
  141.5 1.0 fusion.40
  142.5 1.7 collective-permute-done.8
  144.5 1.2 copy-done
  145.8 1.9 copy-done.1
  147.6 72.3 %ring_scatter.1 = (f32[64,2816]{1,0:T(8,128)S(1)}, f32[64,1536]{1,0:T(8,128)S(1)}, f32[64,1408]{1,0:T(8,128)S(1)}, f32[64,512]{1,0:T(8,128)S(1)}, f32[64,128]{1,0:T(8,128)S(1)}) custom-call(bf16[1024,2816]{1,0:T(8,128)(2,1)} %convolution_convert_fusion.refs_0_, bf16[1024,1536]{1,0:T(8,128)(2,1)S(1)} %copy-done.1, ...), custom_call_target="tpu_custom_call" | custom-call | tf_op jit(solution)/shard_map/ring_scatter/pallas_call | solution.py:357
  222.3 1.4 copy.64
  (88 shorter events, 17.8 us)
Async XLA Ops:
  0.6 9.6 %copy-start.6 = (bf16[512,64]{0,1:T(8,128)(2,1)S(1)}, bf16[512,64]{0,1:T(8,128)(2,1)}, u32[]{:S(2)}) copy-start(bf16[512,64]{0,1:T(8,128)(2,1)} %param.13) | copy-start | bytes 196612
  0.6 10.4 %copy-start.5 = (bf16[1312,64]{0,1:T(8,128)(2,1)S(1)}, bf16[1312,64]{0,1:T(8,128)(2,1)}, u32[]{:S(2)}) copy-start(bf16[1312,64]{0,1:T(8,128)(2,1)} %param.15) | copy-start | bytes 503812
  1.4 81.7 %collective-permute-start.1 = (f32[128,128]{1,0:T(8,128)S(1)}, f32[128,128]{1,0:T(8,128)S(1)}, u32[]{:S(2)}, u32[]{:S(2)}) collective-permute-start(f32[128,128]{1,0:T(8,128)S(1)} %broadcast_in_dim.27), channel_id=1, source_target_pairs={{0,1},{1,0},{2,3},{3,2},{4,5},{5,4},{6,7},{7,6},{8,9},{9,8},{10,11... | collective-permute-start | bytes 196616 | tf_op jit(solution)/shard_map/ppermute | solution.py:685
  5.5 77.7 %collective-permute-start = (bf16[256,1024]{1,0:T(8,128)(2,1)S(1)}, bf16[256,1024]{1,0:T(8,128)(2,1)S(1)}, u32[]{:S(2)}, u32[]{:S(2)}) collective-permute-start(bf16[256,1024]{1,0:T(8,128)(2,1)S(1)} %pad_maximum_fusion.4), channel_id=1, source_target_pairs={{0,1},{1,0},{2,3},{3,2},{4,5},{5,4},{6,7},{7,6},{8,9},{9,8},{10,11... | collective-permute-start | bytes 1572872 | tf_op jit(solution)/shard_map/ppermute | solution.py:725
  80.1 3.2 %copy-start.2 = (bf16[1,128,1024]{2,1,0:T(8,128)(2,1)S(1)}, bf16[1,128,1024]{2,1,0:T(8,128)(2,1)}, u32[]{:S(2)}) copy-start(bf16[1,128,1024]{2,1,0:T(8,128)(2,1)} %param.9) | copy-start | bytes 786436
  81.9 2.2 copy-start.4
  82.9 22.4 %slice-start = ((s8[8650752]{0:T(1024)(128)(4,1)}), s8[4194304]{0:T(1024)(128)(4,1)S(1)}, s32[]{:S(2)}) async-start(s8[8650752]{0:T(1024)(128)(4,1)} %bitcast.83), calls=%async_computation | async-start | bytes 8388608
  84.1 21.2 %slice-start.1 = ((s8[8650752]{0:T(1024)(128)(4,1)}), s8[4194304]{0:T(1024)(128)(4,1)S(1)}, s32[]{:S(2)}) async-start(s8[8650752]{0:T(1024)(128)(4,1)} %bitcast.83), calls=%async_computation.1 | async-start | bytes 8388608
  85.2 20.1 %slice-start.2 = ((s8[8650752]{0:T(1024)(128)(4,1)}), s8[262144]{0:T(1024)(128)(4,1)S(1)}, s32[]{:S(2)}) async-start(s8[8650752]{0:T(1024)(128)(4,1)} %bitcast.83), calls=%async_computation.2 | async-start | bytes 524288
  88.3 8.7 %collective-permute-start.2 = (bf16[128,1024]{1,0:T(8,128)(2,1)S(1)}, bf16[128,1024]{1,0:T(8,128)(2,1)S(1)}, u32[]{:S(2)}, u32[]{:S(2)}) collective-permute-start(bf16[128,1024]{1,0:T(8,128)(2,1)S(1)} %slice.213), channel_id=1, source_target_pairs={{0,1},{1,0},{2,3},{3,2},{4,5},{5,4},{6,7},{7,6},{8,9},{9,8},{10,11... | collective-permute-start | bytes 786440 | tf_op jit(solution)/shard_map/ppermute | solution.py:690
  97.5 7.8 %collective-permute-start.3 = (bf16[128,1024]{1,0:T(8,128)(2,1)S(1)}, bf16[128,1024]{1,0:T(8,128)(2,1)S(1)}, u32[]{:S(2)}, u32[]{:S(2)}) collective-permute-start(bf16[128,1024]{1,0:T(8,128)(2,1)S(1)} %multiply_convert_fusion.2), channel_id=1, source_target_pairs={{0,1},{1,0},{2,3},{3,2},{4,5},{5,4},{6,7},{7,6},{8,9},{9,8},{10,11... | collective-permute-start | bytes 786440 | tf_op jit(solution)/shard_map/ppermute | solution.py:685
  99.1 7.9 %copy-start.3 = (bf16[1,128,1024]{2,1,0:T(8,128)(2,1)S(1)}, bf16[1,128,1024]{2,1,0:T(8,128)(2,1)}, u32[]{:S(2)}) copy-start(bf16[1,128,1024]{2,1,0:T(8,128)(2,1)} %param.11) | copy-start | bytes 786436
  110.2 6.9 %collective-permute-start.4 = (bf16[128,1024]{1,0:T(8,128)(2,1)S(1)}, bf16[128,1024]{1,0:T(8,128)(2,1)S(1)}, u32[]{:S(2)}, u32[]{:S(2)}) collective-permute-start(bf16[128,1024]{1,0:T(8,128)(2,1)S(1)} %slice.212), channel_id=1, source_target_pairs={{0,1},{1,0},{2,3},{3,2},{4,5},{5,4},{6,7},{7,6},{8,9},{9,8},{10,11... | collective-permute-start | bytes 786440 | tf_op jit(solution)/shard_map/ppermute | solution.py:690
  117.7 7.0 %collective-permute-start.5 = (bf16[128,1024]{1,0:T(8,128)(2,1)S(1)}, bf16[128,1024]{1,0:T(8,128)(2,1)S(1)}, u32[]{:S(2)}, u32[]{:S(2)}) collective-permute-start(bf16[128,1024]{1,0:T(8,128)(2,1)S(1)} %get-tuple-element.76), channel_id=1, source_target_pairs={{0,1},{1,0},{2,3},{3,2},{4,5},{5,4},{6,7},{7,6},{8,9},{9,8},{10,11... | collective-permute-start | bytes 786440 | tf_op jit(solution)/shard_map/ppermute | solution.py:685
  125.3 6.4 %collective-permute-start.6 = (bf16[128,1024]{1,0:T(8,128)(2,1)S(1)}, bf16[128,1024]{1,0:T(8,128)(2,1)S(1)}, u32[]{:S(2)}, u32[]{:S(2)}) collective-permute-start(bf16[128,1024]{1,0:T(8,128)(2,1)S(1)} %slice.211), channel_id=1, source_target_pairs={{0,1},{1,0},{2,3},{3,2},{4,5},{5,4},{6,7},{7,6},{8,9},{9,8},{10,11... | collective-permute-start | bytes 786440 | tf_op jit(solution)/shard_map/ppermute | solution.py:690
  133.7 6.5 %collective-permute-start.7 = (bf16[128,1024]{1,0:T(8,128)(2,1)S(1)}, bf16[128,1024]{1,0:T(8,128)(2,1)S(1)}, u32[]{:S(2)}, u32[]{:S(2)}) collective-permute-start(bf16[128,1024]{1,0:T(8,128)(2,1)S(1)} %slice.210), channel_id=1, source_target_pairs={{0,1},{1,0},{2,3},{3,2},{4,5},{5,4},{6,7},{7,6},{8,9},{9,8},{10,11... | collective-permute-start | bytes 786440 | tf_op jit(solution)/shard_map/ppermute | solution.py:690
  140.5 3.7 %collective-permute-start.8 = (f32[2,1024]{1,0:T(2,128)S(1)}, f32[2,1024]{1,0:T(2,128)S(1)}, u32[]{:S(2)}, u32[]{:S(2)}) collective-permute-start(f32[2,1024]{1,0:T(2,128)S(1)} %pad_maximum_fusion.17), channel_id=1, source_target_pairs={{0,1},{1,0},{2,3},{3,2},{4,5},{5,4},{6,7},{7,6},{8,9},{9,8},{10,11... | collective-permute-start | bytes 24584 | tf_op jit(solution)/shard_map/ppermute | solution.py:698
  144.5 1.2 copy-start
  145.8 1.9 copy-start.1
